TPU v7x, 32 devices: a whole 2x2x4 slice. The times are simulated.
32 devices in a mesh: ctx: 8 (over z, x), fsdp: 4 (over y, core).
Axes of the slice: x: 2, y: 2, z: 4, core: 2. Of those that a mesh axis runs over, the one named last changes fastest.
Arguments:
- inputs: bfloat16 [8, 512, 1024], P('fsdp', 'ctx'), may hold values from -6 to 6
- gain_one: bfloat16 [1024], P('fsdp'), may hold values from 0.25 to 1.75
- w_qkv: bfloat16 [1024, 3072], P('fsdp')
- w_attn: bfloat16 [1024, 1024], P('fsdp'), may hold values from -0.75 to 0.75
- gain_two: bfloat16 [1024], P('fsdp'), may hold values from 0.25 to 1.75
- w_in: bfloat16 [1024, 5248], P('fsdp'), may hold values from -0.1875 to 0.1875
- w_ffn: bfloat16 [2624, 1024], P('fsdp'), may hold values from -0.125 to 0.125
- cotangent: bfloat16 [8, 512, 1024], P('fsdp', 'ctx'), may hold values from -6 to 6
Outputs:
- output: bfloat16 [8, 512, 1024], P('fsdp', 'ctx')
- grad_input: float32 [8, 512, 1024], P('fsdp', 'ctx')
- grad_gain_one: float32 [1024], P('fsdp')
- grad_w_qkv: float32 [1024, 3072], P('fsdp')
- grad_w_attn: float32 [1024, 1024], P('fsdp')
- grad_gain_two: float32 [1024], P('fsdp')
- grad_w_in: float32 [1024, 5248], P('fsdp')
- grad_w_ffn: float32 [2624, 1024], P('fsdp')
All inputs are finite; a program needn't handle non-finite values.
Results may differ from a plain program's by a relative error of at most 0.023.
Values may be sent and summed in bfloat16 or wider, within the bound.
A program may use at most 256 MiB of HBM per device.

v0:
```python
import math

import jax
import jax.numpy as jnp
from jax import lax
from jax.sharding import PartitionSpec as P

D = 1024
HEADS = 16
HEAD_DIM = 64
FF = 2624


EPSILON = 1e-05
ROPE_THETA = 160000.0


def norm_parts(values_in):
    mean_val = jnp.mean(values_in, axis=-1, keepdims=True)
    centred = values_in - mean_val
    variance = jnp.mean(centred * centred, axis=-1, keepdims=True)
    inv_std = lax.rsqrt(variance + EPSILON)
    return (centred * inv_std, inv_std)


def norm_back(grad_normed, normed, inv_std):
    return inv_std * (
        grad_normed
        - jnp.mean(grad_normed, axis=-1, keepdims=True)
        - normed * jnp.mean(grad_normed * normed, axis=-1, keepdims=True)
    )


def rotary_tables(positions):
    half_dim = HEAD_DIM // 2
    inv_freq = ROPE_THETA ** (-(jnp.arange(half_dim, dtype=jnp.float32) * 2.0) / HEAD_DIM)
    angles = positions.astype(jnp.float32)[:, None] * inv_freq[None, :]
    cosine = jnp.concatenate([jnp.cos(angles), jnp.cos(angles)], axis=-1)[:, None, :]
    sine_part = jnp.concatenate([jnp.sin(angles), jnp.sin(angles)], axis=-1)[:, None, :]
    return (cosine, sine_part)


def rotate(values_in, cosine, sine_part):
    half_dim = values_in.shape[-1] // 2
    turned = jnp.concatenate([-values_in[..., half_dim:], values_in[..., :half_dim]], axis=-1)
    return values_in * cosine + turned * sine_part


def rotate_back(grads, cosine, sine_part):
    half_dim = grads.shape[-1] // 2
    scaled = grads * sine_part
    turned = jnp.concatenate([scaled[..., half_dim:], -scaled[..., :half_dim]], axis=-1)
    return grads * cosine + turned


def gelu_slope(inner_part):
    cumulative = 0.5 * (1.0 + jax.scipy.special.erf(inner_part * 0.7071067811865476))
    density = jnp.exp(-0.5 * inner_part * inner_part) * 0.3989422804014327
    return cumulative + inner_part * density


def attend_piece(state_in, queries, key_piece, value_piece, scale_factor):
    row_max, row_sum, weighted = state_in
    scores = (
        jnp.einsum("bthd,bshd->bths", queries, key_piece, preferred_element_type=jnp.float32)
        * scale_factor
    )
    new_max = jnp.maximum(row_max, jnp.max(scores, axis=-1))
    rescale = jnp.exp(row_max - new_max)
    exp_vals = jnp.exp(scores - new_max[..., None])
    row_sum = row_sum * rescale + jnp.sum(exp_vals, axis=-1)
    weighted = weighted * rescale[..., None] + jnp.einsum(
        "bths,bshd->bthd",
        exp_vals.astype(jnp.bfloat16),
        value_piece,
        preferred_element_type=jnp.float32,
    )
    return (new_max, row_sum, weighted)


def back_piece(queries, grad_mixed, log_sum, row_delta, key_piece, value_piece, scale_factor):
    scores = (
        jnp.einsum("bthd,bshd->bths", queries, key_piece, preferred_element_type=jnp.float32)
        * scale_factor
    )
    probs = jnp.exp(scores - log_sum[..., None])
    grad_values = jnp.einsum(
        "bths,bthd->bshd",
        probs.astype(jnp.bfloat16),
        grad_mixed,
        preferred_element_type=jnp.float32,
    )
    grad_probs = jnp.einsum(
        "bthd,bshd->bths", grad_mixed, value_piece, preferred_element_type=jnp.float32
    )
    grad_scores = (probs * (grad_probs - row_delta[..., None])).astype(jnp.bfloat16)
    grad_query = (
        jnp.einsum("bths,bshd->bthd", grad_scores, key_piece, preferred_element_type=jnp.float32)
        * scale_factor
    )
    grad_keys = (
        jnp.einsum("bths,bthd->bshd", grad_scores, queries, preferred_element_type=jnp.float32)
        * scale_factor
    )
    return (grad_query, grad_keys, grad_values)


def add_at(whole_grads, piece_grads, offset):
    old_part = lax.dynamic_slice_in_dim(whole_grads, offset, piece_grads.shape[1], 1)
    return lax.dynamic_update_slice_in_dim(whole_grads, old_part + piece_grads, offset, 1)


def on_device(inputs, gain_one, w_qkv, w_attn, gain_two, w_in, w_ffn, cotangent):
    seq_dev = inputs.shape[0]
    tok_seq = inputs.shape[1]
    row_count = seq_dev * tok_seq
    seq_len = tok_seq * lax.axis_size("ctx")
    tokens_f = inputs.reshape(row_count, D).astype(jnp.float32)
    grad_out = cotangent.reshape(row_count, D)
    scale_factor = HEAD_DIM ** (-0.5)
    block_len = math.gcd(seq_len, 512)
    blocks_num = seq_len // block_len
    gathered = (
        lax.all_gather(gain_one, "fsdp", axis=0, tiled=True),
        lax.all_gather(w_qkv, "fsdp", axis=0, tiled=True),
        lax.all_gather(w_attn, "fsdp", axis=0, tiled=True),
        lax.all_gather(gain_two, "fsdp", axis=0, tiled=True),
        lax.all_gather(w_in, "fsdp", axis=0, tiled=True),
        lax.all_gather(w_ffn, "fsdp", axis=0, tiled=True),
    )
    full_g1, full_qkv, full_attn, full_g2, full_in, full_ffn = gathered
    normed_one, inv_one = norm_parts(tokens_f)
    input_one = (normed_one * full_g1.astype(jnp.float32)).astype(jnp.bfloat16)
    project = jnp.dot(input_one, full_qkv, preferred_element_type=jnp.float32)
    positions = lax.axis_index("ctx") * tok_seq + jnp.arange(tok_seq, dtype=jnp.int32)
    cosine, sine_part = rotary_tables(positions)
    shaped = project.reshape(seq_dev, tok_seq, 3, HEADS, HEAD_DIM)
    queries = rotate(shaped[:, :, 0], cosine, sine_part).astype(jnp.bfloat16)
    key_rows = rotate(shaped[:, :, 1], cosine, sine_part).astype(jnp.bfloat16)
    value_rows = shaped[:, :, 2].astype(jnp.bfloat16)
    start_state = (
        jnp.full((seq_dev, tok_seq, HEADS), -jnp.inf, jnp.float32),
        jnp.zeros((seq_dev, tok_seq, HEADS), jnp.float32),
        jnp.zeros((seq_dev, tok_seq, HEADS, HEAD_DIM), jnp.float32),
    )
    whole_keys, whole_values = (
        lax.all_gather(key_rows, "ctx", axis=1, tiled=True),
        lax.all_gather(value_rows, "ctx", axis=1, tiled=True),
    )

    def forward_step(state_in, block_index):
        begin = block_index * block_len
        key_piece = lax.dynamic_slice_in_dim(whole_keys, begin, block_len, 1)
        value_piece = lax.dynamic_slice_in_dim(whole_values, begin, block_len, 1)
        return (attend_piece(state_in, queries, key_piece, value_piece, scale_factor), None)

    state_out, unused = lax.scan(forward_step, start_state, jnp.arange(blocks_num, dtype=jnp.int32))
    row_max, row_sum, weighted = state_out
    attn_f = weighted / row_sum[..., None]
    log_sum = row_max + jnp.log(row_sum)
    attn_b = attn_f.reshape(row_count, D).astype(jnp.bfloat16)
    resid = tokens_f + jnp.dot(attn_b, full_attn, preferred_element_type=jnp.float32)
    normed_two, inv_two = norm_parts(resid)
    input_two = (normed_two * full_g2.astype(jnp.float32)).astype(jnp.bfloat16)
    widened = jnp.dot(input_two, full_in, preferred_element_type=jnp.float32)
    inner_part = widened[:, :FF]
    gating = widened[:, FF:]
    activated = jax.nn.gelu(inner_part, approximate=False)
    hidden = (activated * gating).astype(jnp.bfloat16)
    output = (resid + jnp.dot(hidden, full_ffn, preferred_element_type=jnp.float32)).astype(
        jnp.bfloat16
    )
    back_g1, back_qkv, back_attn, back_g2, back_in, back_ffn = gathered
    grad_ffn = jnp.dot(hidden.T, grad_out, preferred_element_type=jnp.float32)
    grad_hidden = jnp.dot(grad_out, back_ffn.T, preferred_element_type=jnp.float32)
    grad_inner = grad_hidden * gating * gelu_slope(inner_part)
    grad_gating = grad_hidden * activated
    grad_wide = jnp.concatenate([grad_inner, grad_gating], axis=-1).astype(jnp.bfloat16)
    grad_in = jnp.dot(input_two.T, grad_wide, preferred_element_type=jnp.float32)
    grad_normed_two = jnp.dot(grad_wide, back_in.T, preferred_element_type=jnp.float32)
    grad_g2 = jnp.sum(grad_normed_two * normed_two, axis=0)
    grad_resid = grad_out.astype(jnp.float32) + norm_back(
        grad_normed_two * back_g2.astype(jnp.float32), normed_two, inv_two
    )
    part_g2, part_in, part_ffn = (
        lax.psum_scatter(
            grad_g2.astype(jnp.bfloat16), "fsdp", scatter_dimension=0, tiled=True
        ).astype(jnp.float32),
        lax.psum_scatter(
            grad_in.astype(jnp.bfloat16), "fsdp", scatter_dimension=0, tiled=True
        ).astype(jnp.float32),
        lax.psum_scatter(
            grad_ffn.astype(jnp.bfloat16), "fsdp", scatter_dimension=0, tiled=True
        ).astype(jnp.float32),
    )
    resid_b = grad_resid.astype(jnp.bfloat16)
    grad_attn_w = jnp.dot(attn_b.T, resid_b, preferred_element_type=jnp.float32)
    grad_mixed = (
        jnp.dot(resid_b, back_attn.T, preferred_element_type=jnp.float32)
        .astype(jnp.bfloat16)
        .reshape(seq_dev, tok_seq, HEADS, HEAD_DIM)
    )
    row_delta = jnp.sum(grad_mixed.astype(jnp.float32) * attn_f, axis=-1)
    zero_q = jnp.zeros((seq_dev, tok_seq, HEADS, HEAD_DIM), jnp.float32)
    zero_kv = jnp.zeros((seq_dev, seq_len, HEADS, HEAD_DIM), jnp.float32)

    def backward_step(state_in, block_index):
        grad_q_sum, grad_key_all, grad_value_all = state_in
        begin = block_index * block_len
        key_piece = lax.dynamic_slice_in_dim(whole_keys, begin, block_len, 1)
        value_piece = lax.dynamic_slice_in_dim(whole_values, begin, block_len, 1)
        grad_query, grad_keys, grad_values = back_piece(
            queries, grad_mixed, log_sum, row_delta, key_piece, value_piece, scale_factor
        )
        return (
            (
                grad_q_sum + grad_query,
                add_at(grad_key_all, grad_keys, begin),
                add_at(grad_value_all, grad_values, begin),
            ),
            None,
        )

    back_state, unused_back = lax.scan(
        backward_step, (zero_q, zero_kv, zero_kv), jnp.arange(blocks_num, dtype=jnp.int32)
    )
    grad_q_sum, grad_key_all, grad_value_all = back_state
    own_keys, own_values = (
        lax.psum_scatter(
            grad_key_all.astype(jnp.bfloat16), "ctx", scatter_dimension=1, tiled=True
        ).astype(jnp.float32),
        lax.psum_scatter(
            grad_value_all.astype(jnp.bfloat16), "ctx", scatter_dimension=1, tiled=True
        ).astype(jnp.float32),
    )
    grad_q_rot = rotate_back(grad_q_sum, cosine, sine_part).reshape(row_count, D)
    grad_k_rot = rotate_back(own_keys, cosine, sine_part).reshape(row_count, D)
    grad_joint = jnp.concatenate(
        [grad_q_rot, grad_k_rot, own_values.reshape(row_count, D)], axis=-1
    ).astype(jnp.bfloat16)
    grad_qkv = jnp.dot(input_one.T, grad_joint, preferred_element_type=jnp.float32)
    grad_normed_one = jnp.dot(grad_joint, back_qkv.T, preferred_element_type=jnp.float32)
    grad_g1 = jnp.sum(grad_normed_one * normed_one, axis=0)
    grad_input = grad_resid + norm_back(
        grad_normed_one * back_g1.astype(jnp.float32), normed_one, inv_one
    )
    part_g1, part_qkv, part_attn = (
        lax.psum_scatter(
            grad_g1.astype(jnp.bfloat16), "fsdp", scatter_dimension=0, tiled=True
        ).astype(jnp.float32),
        lax.psum_scatter(
            grad_qkv.astype(jnp.bfloat16), "fsdp", scatter_dimension=0, tiled=True
        ).astype(jnp.float32),
        lax.psum_scatter(
            grad_attn_w.astype(jnp.bfloat16), "fsdp", scatter_dimension=0, tiled=True
        ).astype(jnp.float32),
    )
    totals = (
        lax.psum(part_g1.astype(jnp.bfloat16), "ctx").astype(jnp.float32),
        lax.psum(part_qkv.astype(jnp.bfloat16), "ctx").astype(jnp.float32),
        lax.psum(part_attn.astype(jnp.bfloat16), "ctx").astype(jnp.float32),
        lax.psum(part_g2.astype(jnp.bfloat16), "ctx").astype(jnp.float32),
        lax.psum(part_in.astype(jnp.bfloat16), "ctx").astype(jnp.float32),
        lax.psum(part_ffn.astype(jnp.bfloat16), "ctx").astype(jnp.float32),
    )
    return (
        output.reshape(seq_dev, tok_seq, D),
        grad_input.reshape(seq_dev, tok_seq, D),
        totals[0],
        totals[1],
        totals[2],
        totals[3],
        totals[4],
        totals[5],
    )


def solution(mesh):
    return jax.shard_map(
        on_device,
        mesh=mesh,
        in_specs=(
            P("fsdp", "ctx", None),
            P("fsdp"),
            P("fsdp", None),
            P("fsdp", None),
            P("fsdp"),
            P("fsdp", None),
            P("fsdp", None),
            P("fsdp", "ctx", None),
        ),
        out_specs=(
            P("fsdp", "ctx", None),
            P("fsdp", "ctx", None),
            P("fsdp"),
            P("fsdp", None),
            P("fsdp", None),
            P("fsdp"),
            P("fsdp", None),
            P("fsdp", None),
        ),
        check_vma=False,
    )
```

profile of v0, /device:TPU:0, one launch (start us, length us, event | category | flops | bytes accessed | tf_op | source)
XLA Modules:
  0.0 1007.4 jit_solution(11697671415666420469)
XLA Ops:
  8.6 6.0 all-gather.1
  16.9 41.8 %all-gather.10.cloned.1.call-done = bf16[1024,3072]{1,0:T(8,128)(2,1)} async-done(((bf16[256,3072]{1,0:T(8,128)(2,1)}), bf16[1024,3072]{1,0:T(8,128)(2,1)}) %all-gather.10.cloned.1.call-update) | async-done | bytes 6291472 | tf_op jit(solution)/shard_map/all_gather | solution.py:125
  58.7 8.7 copy.36
  67.4 4.7 fusion.61
  83.7 5.2 all-gather.2
  89.0 59.3 %all-gather.20.cloned.1.call-done = bf16[2,512,1,16,64]{4,3,2,0,1:T(8,128)(2,1)} async-done(((bf16[2,64,1,16,64]{4,3,2,0,1:T(8,128)(2,1)}), bf16[2,512,1,16,64]{4,3,2,0,1:T(8,128)(2,1)}) %all-gather.20.cloned.1.call-update) | async-done | bytes 2097168 | tf_op jit(solution)/shard_map/all_gather | solution.py:148
  148.3 5.4 copy.42
  153.7 68.6 %all-gather.12.cloned.1.call-done = bf16[2,512,16,64]{3,2,0,1:T(8,128)(2,1)} async-done(((bf16[2,64,16,64]{3,2,0,1:T(8,128)(2,1)}), bf16[2,512,16,64]{3,2,0,1:T(8,128)(2,1)}) %all-gather.12.cloned.1.call-update) | async-done | bytes 2097168 | tf_op jit(solution)/shard_map/all_gather | solution.py:147
  222.4 4.5 copy.48
  233.8 11.1 %all-gather.14.cloned.1.call-done = bf16[1024,1024]{1,0:T(8,128)(2,1)} async-done(((bf16[256,1024]{1,0:T(8,128)(2,1)}), bf16[1024,1024]{1,0:T(8,128)(2,1)}) %all-gather.14.cloned.1.call-update) | async-done | bytes 2097168 | tf_op jit(solution)/shard_map/all_gather | solution.py:126
  247.3 70.8 %all-gather.16.cloned.1.call-done = bf16[1024,5248]{1,0:T(8,128)(2,1)} async-done(((bf16[256,5248]{1,0:T(8,128)(2,1)}), bf16[1024,5248]{1,0:T(8,128)(2,1)}) %all-gather.16.cloned.1.call-update) | async-done | bytes 10747920 | tf_op jit(solution)/shard_map/all_gather | solution.py:128
  318.0 7.3 fusion.73
  325.3 35.3 %all-gather.18.cloned.1.call-done = bf16[2624,1024]{1,0:T(8,128)(2,1)} async-done(((bf16[656,1024]{1,0:T(8,128)(2,1)}), bf16[2624,1024]{1,0:T(8,128)(2,1)}) %all-gather.18.cloned.1.call-update) | async-done | bytes 5373968 | tf_op jit(solution)/shard_map/all_gather | solution.py:129
  360.6 8.5 multiply_convert_fusion.1
  378.9 4.2 fusion.1
  386.5 7.4 copy.56
  393.9 6.8 reshape.175
  400.7 4.4 convert_bitcast_fusion
  405.2 7.4 copy.58
  412.6 6.8 reshape.177
  433.2 36.0 %reduce-scatter.19.cloned.1.call-done = bf16[64,2048]{1,0:T(8,128)(2,1)} async-done(((bf16[512,2048]{1,0:T(8,128)(2,1)}), bf16[64,2048]{1,0:T(8,128)(2,1)}) %reduce-scatter.19.cloned.1.call-update) | async-done | bytes 262160
  473.2 67.0 %reduce-scatter.21.cloned.1.call-done = bf16[64,2048]{1,0:T(8,128)(2,1)} async-done(((bf16[512,2048]{1,0:T(8,128)(2,1)}), bf16[64,2048]{1,0:T(8,128)(2,1)}) %reduce-scatter.21.cloned.1.call-update) | async-done | bytes 262160
  543.0 5.1 multiply_reduce_fusion.2
  548.1 4.4 convolution_convert_fusion.2
  553.7 7.0 convolution_convert_fusion
  560.8 12.2 %reduce-scatter.13.cloned.1.call-done = bf16[256,1024]{1,0:T(8,128)(2,1)} async-done(((bf16[1024,1024]{1,0:T(8,128)(2,1)}), bf16[256,1024]{1,0:T(8,128)(2,1)}) %reduce-scatter.13.cloned.1.call-update) | async-done | bytes 524304 | tf_op jit(solution)/shard_map/reduce_scatter | solution.py:254
  573.0 55.2 %reduce-scatter.17.cloned.1.call-done = bf16[656,1024]{1,0:T(8,128)(2,1)} async-done(((bf16[2624,1024]{1,0:T(8,128)(2,1)}), bf16[656,1024]{1,0:T(8,128)(2,1)}) %reduce-scatter.17.cloned.1.call-update) | async-done | bytes 1343504 | tf_op jit(solution)/shard_map/reduce_scatter | solution.py:192
  628.2 61.4 %reduce-scatter.11.cloned.1.call-done = bf16[256,3072]{1,0:T(8,128)(2,1)} async-done(((bf16[1024,3072]{1,0:T(8,128)(2,1)}), bf16[256,3072]{1,0:T(8,128)(2,1)}) %reduce-scatter.11.cloned.1.call-update) | async-done | bytes 1572880 | tf_op jit(solution)/shard_map/reduce_scatter | solution.py:251
  689.6 88.5 %reduce-scatter.15.cloned.1.call-done = bf16[256,5248]{1,0:T(8,128)(2,1)} async-done(((bf16[1024,5248]{1,0:T(8,128)(2,1)}), bf16[256,5248]{1,0:T(8,128)(2,1)}) %reduce-scatter.15.cloned.1.call-update) | async-done | bytes 2686992 | tf_op jit(solution)/shard_map/reduce_scatter | solution.py:189
  784.2 5.7 all-reduce.4
  790.1 22.7 %all-reduce.2 = (bf16[256]{0:T(256)(128)(2,1)S(1)}, bf16[256]{0:T(256)(128)(2,1)S(1)}) all-reduce(bf16[256]{0:T(256)(128)(2,1)S(1)} %dynamic-slice.1, bf16[256]{0:T(256)(128)(2,1)S(1)} %dynamic-slice.3), channel_id=1, replica_groups=mesh['ctx'=8,'fsdp'=4] {'ctx'}, use_global_device_ids=true, to_apply=%region_15.16 | all-reduce | flops 512 | bytes 2048 | tf_op jit(solution)/shard_map/psum | solution.py:259
  815.0 175.5 %all-reduce.7.cloned.1.call-done = (bf16[256,3072]{1,0:T(8,128)(2,1)}, bf16[256,1024]{1,0:T(8,128)(2,1)}, bf16[256,5248]{1,0:T(8,128)(2,1)}, bf16[656,1024]{1,0:T(8,128)(2,1)}) async-done(((bf16[256,3072]{1,0:T(8,128)(2,1)}, bf16[256,1024]{1,0:T(8,128)(2,1)}, bf16[256,5248]{1,0:T(8,128)(2,1)}, bf16[656,1024]{1,0:T(8,128)(2,1)}), (bf16[256,3072]{1,0:T(8,128)(2,1)}, bf16[256,1024]{1,0:T(8,128)(2,1)}, ...) | async-done | bytes 6127632 | tf_op jit(solution)/shard_map/psum | solution.py:260
  (150 shorter events, 76.7 us)
Async XLA Ops:
  7.2 51.5 %all-gather.10.cloned.1.call-start = ((), (), s32[]{:S(2)}) async-start(), calls=%async_computation.6 | async-start | bytes 7864320 | tf_op jit(solution)/shard_map/all_gather | solution.py:125
  7.9 140.4 %all-gather.20.cloned.1.call-start = ((), (), s32[]{:S(2)}) async-start(), calls=%async_computation.15 | async-start | bytes 4718592 | tf_op jit(solution)/shard_map/all_gather | solution.py:148
  58.7 8.7 copy-start.10
  72.1 1.7 copy-start.8
  75.4 146.9 %all-gather.12.cloned.1.call-start = ((), (), s32[]{:S(2)}) async-start(), calls=%async_computation.7 | async-start | bytes 4718592 | tf_op jit(solution)/shard_map/all_gather | solution.py:147
  78.0 1.9 copy-start.9
  80.4 146.5 %copy-start.12 = (bf16[2,64,16,64]{1,3,2,0:T(8,128)(2,1)}, bf16[2,64,16,64]{1,3,2,0:T(8,128)(2,1)S(1)}, u32[]{:S(2)}) copy-start(bf16[2,64,16,64]{1,3,2,0:T(8,128)(2,1)S(1)} %get-tuple-element.76) | copy-start | bytes 786436
  81.9 163.0 %all-gather.14.cloned.1.call-start = ((), (), s32[]{:S(2)}) async-start(), calls=%async_computation.8 | async-start | bytes 2621440 | tf_op jit(solution)/shard_map/all_gather | solution.py:126
  82.5 235.5 %all-gather.16.cloned.1.call-start = ((), (), s32[]{:S(2)}) async-start(), calls=%async_computation.9 | async-start | bytes 13434880 | tf_op jit(solution)/shard_map/all_gather | solution.py:128
  83.1 277.5 %all-gather.18.cloned.1.call-start = ((), (), s32[]{:S(2)}) async-start(), calls=%async_computation.10 | async-start | bytes 6717440 | tf_op jit(solution)/shard_map/all_gather | solution.py:129
  83.7 385.5 %reduce-scatter.19.cloned.1.call-start = ((), (), s32[]{:S(2)}) async-start(), calls=%async_computation.16 | async-start | bytes 2359296
  227.7 2.2 copy-start
  227.7 3.2 copy-start.3
  318.0 42.6 %copy-start.17 = (bf16[2,64,1024]{2,1,0:T(8,128)(2,1)S(1)}, bf16[2,64,1024]{2,1,0:T(8,128)(2,1)}, u32[]{:S(2)}) copy-start(bf16[2,64,1024]{2,1,0:T(8,128)(2,1)} %param.15) | copy-start | bytes 786436
  360.6 8.5 copy-start.2
  369.1 3.7 copy-start.19
  369.1 3.7 copy-start.21
  369.2 4.8 copy-start.4
  378.9 5.6 copy-start.13
  383.1 1.3 copy-start.1
  400.7 139.5 %reduce-scatter.21.cloned.1.call-start = ((), (), s32[]{:S(2)}) async-start(), calls=%async_computation.17 | async-start | bytes 2359296
  419.4 153.6 %reduce-scatter.13.cloned.1.call-start = ((), (), s32[]{:S(2)}) async-start(), calls=%async_computation.12 | async-start | bytes 2621440 | tf_op jit(solution)/shard_map/reduce_scatter | solution.py:254
  422.5 205.7 %reduce-scatter.17.cloned.1.call-start = ((), (), s32[]{:S(2)}) async-start(), calls=%async_computation.14 | async-start | bytes 6717440 | tf_op jit(solution)/shard_map/reduce_scatter | solution.py:192
  422.6 2.3 copy-start.18
  428.9 260.7 %reduce-scatter.11.cloned.1.call-start = ((), (), s32[]{:S(2)}) async-start(), calls=%async_computation.11 | async-start | bytes 7864320 | tf_op jit(solution)/shard_map/reduce_scatter | solution.py:251
  472.2 70.9 %copy-start.11 = (bf16[2,64,1024]{2,1,0:T(8,128)(2,1)S(1)}, bf16[2,64,1024]{2,1,0:T(8,128)(2,1)}, u32[]{:S(2)}) copy-start(bf16[2,64,1024]{2,1,0:T(8,128)(2,1)} %param.8) | copy-start | bytes 786436
  552.6 225.5 %reduce-scatter.15.cloned.1.call-start = ((), (), s32[]{:S(2)}) async-start(), calls=%async_computation.13 | async-start | bytes 13434880 | tf_op jit(solution)/shard_map/reduce_scatter | solution.py:189
  560.7 429.9 %all-reduce.7.cloned.1.call-start = ((), (), s32[]{:S(2)}) async-start(), calls=%async_computation.18 | async-start | bytes 12255232 | tf_op jit(solution)/shard_map/psum | solution.py:260
  780.0 34.0 %copy-start.7 = (f32[128,1024]{1,0:T(8,128)S(1)}, f32[128,1024]{1,0:T(8,128)}, u32[]{:S(2)}) copy-start(f32[128,1024]{1,0:T(8,128)} %copy-done.5) | copy-start | bytes 1572868
  990.6 2.2 copy-start.15
  992.8 2.0 copy-start.16
  994.9 2.7 copy-start.14
  (6 other events, 5.6 us)
Sparse Core Ops, SparseCore 0:
  9.5 49.1 all-gather.9
  75.5 72.7 all-gather.19
  151.0 71.3 all-gather.11
  223.8 21.0 all-gather.13
  246.3 71.6 all-gather.15
  319.4 41.1 all-gather.17
  400.8 68.3 reduce-scatter.18
  472.7 67.3 reduce-scatter.20
  542.7 30.2 reduce-scatter.12
  576.0 52.1 reduce-scatter.16
  630.7 58.8 reduce-scatter.10
  692.1 85.9 reduce-scatter.14
  782.8 207.7 all-reduce.6
where the time goes:
time: 1010 us
  waiting for transfers between devices  785 us (78%)
  local copies, waits for them, and re-layouts  75 us (7%)
  matrix products  70 us (7%)
  blocking collectives  39.8 us (4%)
  other arithmetic  20.9 us (2%)
  between operations  15.5 us (2%)
    psum x1, waiting for transfers between devices, on_device(): lax.psum(part_qkv.astype(jnp.bfloat16), 'ctx').astype(jnp.float32)  176 us
    unnamed x15, waiting for transfers between devices  105 us
    reduce_scatter x1, waiting for transfers between devices, on_device(): lax.psum_scatter(grad_in.astype(jnp.bfloat16), 'fsdp', scatter_dimension=...  88.5 us
    all_gather x1, waiting for transfers between devices, on_device(): lax.all_gather(w_in, 'fsdp', axis=0, tiled=True)  70.8 us
    all_gather x1, waiting for transfers between devices, on_device(): lax.all_gather(key_rows, 'ctx', axis=1, tiled=True)  68.6 us
    reduce_scatter x1, waiting for transfers between devices, on_device(): lax.psum_scatter(grad_qkv.astype(jnp.bfloat16), 'fsdp', scatter_dimension...  61.4 us
    all_gather x1, waiting for transfers between devices, on_device(): lax.all_gather(value_rows, 'ctx', axis=1, tiled=True)  59.3 us
    reduce_scatter x1, waiting for transfers between devices, on_device(): lax.psum_scatter(grad_ffn.astype(jnp.bfloat16), 'fsdp', scatter_dimension...  55.2 us
  transfers between devices with their start and end apart: 13, of which 13 were waited for; matrix products, arithmetic and copies ran while one was open for 9% of the time, Pallas kernels for 0%

commit v1 on v0

--- a/solution.py
+++ b/solution.py
@@ -275,9 +275,193 @@
     )
 
 
+def gather_tokens(rows):
+    return lax.all_gather(rows, "ctx", axis=0, tiled=True)
+
+
+def scatter_tokens(partial_rows):
+    return lax.psum_scatter(
+        partial_rows.astype(jnp.bfloat16), "ctx", scatter_dimension=0, tiled=True
+    ).astype(jnp.float32)
+
+
+def by_heads(inputs, gain_one, w_qkv, w_attn, gain_two, w_in, w_ffn, cotangent):
+    blocks = lax.axis_size("ctx")
+    owners = lax.axis_size("fsdp")
+    block = lax.axis_index("ctx")
+    seq_dev, tok_seq, _ = inputs.shape
+    own_rows = seq_dev * tok_seq
+    all_rows = own_rows * blocks
+    seq_len = tok_seq * blocks
+    row_part = w_qkv.shape[0]
+    head_cols = D // blocks
+    heads_dev = HEADS // blocks
+    unit_dev = FF // blocks
+    scale_factor = HEAD_DIM ** (-0.5)
+    f32, bf16 = jnp.float32, jnp.bfloat16
+
+    own_x = inputs.reshape(own_rows, D)
+    own_cot = cotangent.reshape(own_rows, D)
+
+    qkv_part = lax.dynamic_slice_in_dim(
+        w_qkv.reshape(row_part, 3, D), block * head_cols, head_cols, 2
+    ).reshape(row_part, 3 * head_cols)
+    in_part = jnp.concatenate(
+        [
+            lax.dynamic_slice_in_dim(w_in, block * unit_dev, unit_dev, 1),
+            lax.dynamic_slice_in_dim(w_in, FF + block * unit_dev, unit_dev, 1),
+        ],
+        axis=1,
+    )
+    packed = jnp.concatenate([qkv_part, gain_one[:, None], gain_two[:, None]], axis=1)
+    packed = lax.all_gather(packed, "fsdp", axis=0, tiled=True)
+    qkv_c = packed[:, : 3 * head_cols]
+    full_g1 = packed[:, 3 * head_cols].astype(f32)
+    full_g2 = packed[:, 3 * head_cols + 1].astype(f32)
+    all_x = gather_tokens(own_x)
+    full_attn = lax.all_gather(w_attn, "fsdp", axis=0, tiled=True)
+    in_c = lax.all_gather(in_part, "fsdp", axis=0, tiled=True)
+    ffn_cols = lax.all_to_all(w_ffn, "fsdp", split_axis=1, concat_axis=0, tiled=True)
+    ffn_c = lax.all_gather(
+        lax.dynamic_slice_in_dim(ffn_cols, block * unit_dev, unit_dev, 0),
+        "fsdp",
+        axis=1,
+        tiled=True,
+    )
+    all_cot = gather_tokens(own_cot)
+
+    normed_all, _ = norm_parts(all_x.astype(f32))
+    input_one = (normed_all * full_g1).astype(bf16)
+    project = jnp.dot(input_one, qkv_c, preferred_element_type=f32)
+    cosine, sine_part = rotary_tables(jnp.arange(seq_len, dtype=jnp.int32))
+    shaped = project.reshape(blocks, seq_dev, tok_seq, 3, heads_dev, HEAD_DIM)
+    shaped = shaped.transpose(3, 1, 0, 2, 4, 5).reshape(3, seq_dev, seq_len, heads_dev, HEAD_DIM)
+    queries = rotate(shaped[0], cosine, sine_part).astype(bf16)
+    key_rows = rotate(shaped[1], cosine, sine_part).astype(bf16)
+    value_rows = shaped[2].astype(bf16)
+    scores = (
+        jnp.einsum("bthd,bshd->bhts", queries, key_rows, preferred_element_type=f32) * scale_factor
+    )
+    row_max = jnp.max(scores, axis=-1, keepdims=True)
+    exp_vals = jnp.exp(scores - row_max)
+    row_sum = jnp.sum(exp_vals, axis=-1, keepdims=True)
+    weighted = jnp.einsum(
+        "bhts,bshd->bhtd", exp_vals.astype(bf16), value_rows, preferred_element_type=f32
+    )
+    attn_f = weighted / row_sum
+    log_sum = row_max + jnp.log(row_sum)
+    attn_b = attn_f.astype(bf16).reshape(seq_dev, heads_dev, blocks, tok_seq, HEAD_DIM)
+    attn_b = attn_b.transpose(2, 0, 3, 1, 4).reshape(blocks, own_rows, head_cols)
+    own_attn = lax.all_to_all(attn_b, "ctx", split_axis=0, concat_axis=0, tiled=True)
+    own_attn = own_attn.transpose(1, 0, 2).reshape(own_rows, D)
+
+    resid = own_x.astype(f32) + jnp.dot(own_attn, full_attn, preferred_element_type=f32)
+    normed_two, inv_two = norm_parts(resid)
+    input_two = gather_tokens((normed_two * full_g2).astype(bf16))
+
+    widened = jnp.dot(input_two, in_c, preferred_element_type=f32)
+    inner_part = widened[:, :unit_dev]
+    gating = widened[:, unit_dev:]
+    activated = jax.nn.gelu(inner_part, approximate=False)
+    hidden = (activated * gating).astype(bf16)
+    grad_hidden = lax.dot_general(
+        all_cot, ffn_c, (((1,), (1,)), ((), ())), preferred_element_type=f32
+    )
+    grad_wide = jnp.concatenate(
+        [grad_hidden * gating * gelu_slope(inner_part), grad_hidden * activated], axis=-1
+    ).astype(bf16)
+    own_grad_two = scatter_tokens(
+        lax.dot_general(grad_wide, in_c, (((1,), (1,)), ((), ())), preferred_element_type=f32)
+    )
+    output = resid + scatter_tokens(jnp.dot(hidden, ffn_c, preferred_element_type=f32))
+
+    grad_in = lax.dot_general(
+        grad_wide, input_two, (((0,), (0,)), ((), ())), preferred_element_type=f32
+    ).astype(bf16)
+    grad_in = lax.psum_scatter(grad_in, "fsdp", scatter_dimension=1, tiled=True)
+    grad_in = lax.all_gather(grad_in, "ctx", axis=0, tiled=False)
+    grad_in = grad_in.reshape(blocks, 2, unit_dev, row_part).transpose(1, 0, 2, 3)
+    grad_in = grad_in.reshape(2 * FF, row_part).T.astype(f32)
+    grad_ffn = lax.dot_general(
+        hidden, all_cot, (((0,), (0,)), ((), ())), preferred_element_type=f32
+    ).astype(bf16)
+    grad_ffn = lax.psum_scatter(grad_ffn, "fsdp", scatter_dimension=1, tiled=True)
+    grad_ffn = lax.all_gather(grad_ffn, "ctx", axis=0, tiled=True)
+    grad_ffn = lax.all_to_all(grad_ffn, "fsdp", split_axis=0, concat_axis=1, tiled=True)
+    grad_ffn = grad_ffn.astype(f32)
+
+    own_resid = own_cot.astype(f32) + norm_back(own_grad_two * full_g2, normed_two, inv_two)
+    resid_b = own_resid.astype(bf16)
+    own_mixed = lax.dot_general(
+        resid_b, full_attn, (((1,), (1,)), ((), ())), preferred_element_type=f32
+    ).astype(bf16)
+    own_mixed = own_mixed.reshape(own_rows, blocks, head_cols).transpose(1, 0, 2)
+    mixed = lax.all_to_all(own_mixed, "ctx", split_axis=0, concat_axis=0, tiled=True)
+    mixed = mixed.reshape(blocks, seq_dev, tok_seq, heads_dev, HEAD_DIM).transpose(1, 3, 0, 2, 4)
+    mixed = mixed.reshape(seq_dev, heads_dev, seq_len, HEAD_DIM)
+    grad_attn = lax.dot_general(
+        own_attn, resid_b, (((0,), (0,)), ((), ())), preferred_element_type=f32
+    ).astype(bf16)
+    grad_attn = lax.psum_scatter(grad_attn, "fsdp", scatter_dimension=0, tiled=True)
+    grad_attn = lax.psum(grad_attn, "ctx").astype(f32)
+
+    row_delta = jnp.sum(mixed.astype(f32) * attn_f, axis=-1, keepdims=True)
+    probs = jnp.exp(scores - log_sum)
+    grad_values = jnp.einsum(
+        "bhts,bhtd->bshd", probs.astype(bf16), mixed, preferred_element_type=f32
+    )
+    grad_probs = jnp.einsum("bhtd,bshd->bhts", mixed, value_rows, preferred_element_type=f32)
+    grad_scores = (probs * (grad_probs - row_delta)).astype(bf16)
+    grad_query = (
+        jnp.einsum("bhts,bshd->bthd", grad_scores, key_rows, preferred_element_type=f32)
+        * scale_factor
+    )
+    grad_keys = (
+        jnp.einsum("bhts,bthd->bshd", grad_scores, queries, preferred_element_type=f32)
+        * scale_factor
+    )
+    joint = jnp.stack(
+        [
+            rotate_back(grad_query, cosine, sine_part),
+            rotate_back(grad_keys, cosine, sine_part),
+            grad_values,
+        ]
+    ).astype(bf16)
+    joint = joint.reshape(3, seq_dev, blocks, tok_seq, head_cols).transpose(2, 1, 3, 0, 4)
+    joint = joint.reshape(all_rows, 3 * head_cols)
+    own_grad_one = scatter_tokens(
+        lax.dot_general(joint, qkv_c, (((1,), (1,)), ((), ())), preferred_element_type=f32)
+    )
+    grad_qkv = lax.dot_general(
+        input_one, joint, (((0,), (0,)), ((), ())), preferred_element_type=f32
+    ).astype(bf16)
+    grad_qkv = lax.psum_scatter(grad_qkv, "fsdp", scatter_dimension=0, tiled=True)
+    grad_qkv = lax.all_gather(grad_qkv, "ctx", axis=0, tiled=False)
+    grad_qkv = grad_qkv.reshape(blocks, row_part, 3, head_cols).transpose(1, 2, 0, 3)
+    grad_qkv = grad_qkv.reshape(row_part, 3 * D).astype(f32)
+    normed_one, inv_one = norm_parts(own_x.astype(f32))
+    grad_input = own_resid + norm_back(own_grad_one * full_g1, normed_one, inv_one)
+
+    grad_g1 = jnp.sum(w_qkv.astype(f32) * grad_qkv, axis=1) / gain_one.astype(f32)
+    grad_g2 = jnp.sum(w_in.astype(f32) * grad_in, axis=1) / gain_two.astype(f32)
+    return (
+        output.astype(bf16).reshape(seq_dev, tok_seq, D),
+        grad_input.reshape(seq_dev, tok_seq, D),
+        grad_g1,
+        grad_qkv,
+        grad_attn,
+        grad_g2,
+        grad_in,
+        grad_ffn,
+    )
+
+
 def solution(mesh):
+    blocks = mesh.shape["ctx"]
+    split_ok = HEADS % blocks == 0 and FF % blocks == 0 and (D // blocks) % 128 == 0
+
     return jax.shard_map(
-        on_device,
+        by_heads if split_ok else on_device,
         mesh=mesh,
         in_specs=(
             P("fsdp", "ctx", None),

time: 1010 us -> 790 us (0.78)
  waiting for transfers between devices: 785 us -> 584 us
  matrix products: 70 us -> 51.6 us
  local copies, waits for them, and re-layouts: 75 us -> 58.1 us
  starting transfers between devices: 1.07 us -> 12.6 us
  blocking collectives: 39.8 us -> 28.9 us
    psum x1, waiting for transfers between devices: 176 us -> 72 us  [by_heads(): grad_attn = lax.psum(grad_attn, 'ctx').astype(f32)]
    unnamed x15 -> x16, waiting for transfers between devices: 105 us -> 2.12 us
    all_gather x6 -> x8, waiting for transfers between devices: 287 us -> 236 us  [the longest x3 101 us: gather_tokens(): return lax.all_gather(rows, 'ctx', axis=0, tiled=True)]
    reduce_scatter x4 -> x7, waiting for transfers between devices: 217 us -> 257 us  [the longest x3 180 us: scatter_tokens(): lax.psum_scatter(partial_rows.astype(jnp.bfloat16), 'ctx', scatter_dimens...]
    unnamed x64 -> x73, local copies, waits for them, and re-layouts: 45.4 us -> 22.2 us
    psum x1 -> x0, blocking collectives: 22.7 us -> none  [on_device(): lax.psum(part_g1.astype(jnp.bfloat16), 'ctx').astype(jnp.float32)]
    dot_general x18, matrix products: 70 us -> 51.6 us  [the longest x1 6.43 us: by_heads(): lax.dot_general(all_cot, ffn_c, (((1,), (1,)), ((), ())), preferred_eleme...]
    all_to_all x0 -> x3, waiting for transfers between devices: none -> 17.5 us  [the longest x1 17.5 us: by_heads(): lax.all_to_all(w_ffn, 'fsdp', split_axis=1, concat_axis=0, tiled=True)]
  transfers between devices with their start and end apart: 13 -> 19, of which waited for: 13 -> 15; matrix products, arithmetic and copies ran while one was open for 9% -> 15% of each run, Pallas kernels for 0% -> 0%
where the time goes in v1:
time: 790 us; the launch traced here: 780 us
  waiting for transfers between devices  584 us (74%)
  local copies, waits for them, and re-layouts  58.1 us (7%)
  matrix products  51.6 us (7%)
  other arithmetic  29.5 us (4%)
  blocking collectives  28.9 us (4%)
  between operations  15.1 us (2%)
  starting transfers between devices  12.6 us (2%)
    reduce_scatter x3, waiting for transfers between devices, scatter_tokens(): lax.psum_scatter(partial_rows.astype(jnp.bfloat16), 'ctx', scatter_dimens...  180 us
    all_gather x3, waiting for transfers between devices, gather_tokens(): return lax.all_gather(rows, 'ctx', axis=0, tiled=True)  101 us
    psum x1, waiting for transfers between devices, by_heads(): grad_attn = lax.psum(grad_attn, 'ctx').astype(f32)  72 us
    all_gather x1, waiting for transfers between devices, by_heads(): grad_in = lax.all_gather(grad_in, 'ctx', axis=0, tiled=False)  47.7 us
    all_gather x1, waiting for transfers between devices, by_heads(): grad_ffn = lax.all_gather(grad_ffn, 'ctx', axis=0, tiled=True)  44.3 us
    all_gather x1, waiting for transfers between devices, by_heads(): grad_qkv = lax.all_gather(grad_qkv, 'ctx', axis=0, tiled=False)  43.3 us
    reduce_scatter x1, waiting for transfers between devices, by_heads(): lax.psum_scatter(grad_attn, 'fsdp', scatter_dimension=0, tiled=True)  31.4 us
    reduce_scatter x1, waiting for transfers between devices, by_heads(): lax.psum_scatter(grad_qkv, 'fsdp', scatter_dimension=0, tiled=True)  22.5 us
  transfers between devices with their start and end apart: 19, of which 15 were waited for; matrix products, arithmetic and copies ran while one was open for 15% of the time, Pallas kernels for 0%

profile of v1, /device:TPU:0, one launch (start us, length us, event | category | flops | bytes accessed | tf_op | source)
XLA Modules:
  0.0 780.2 jit_solution(16054781915341581083)
XLA Ops:
  11.8 10.2 %all_gather.37 = bf16[1024,386]{0,1:T(8,128)(2,1)S(1)} all-gather(bf16[256,386]{0,1:T(8,128)(2,1)S(1)} %pad_maximum_fusion.4), channel_id=1, replica_groups=mesh['ctx'=8,'fsdp'=4] {'fsdp'}, dimensions={0}, use_global_device_ids=true | all-gather | bytes 988160 | tf_op jit(solution)/shard_map/all_gather | solution.py:317
  23.1 38.8 %all-gather.11.cloned.1.call-done = bf16[1024,1024]{1,0:T(8,128)(2,1)} async-done(((bf16[128,1024]{1,0:T(8,128)(2,1)}), bf16[1024,1024]{1,0:T(8,128)(2,1)}) %all-gather.11.cloned.1.call-update) | async-done | bytes 2097168 | tf_op jit(solution)/shard_map/all_gather | solution.py:279
  69.4 3.5 reshape.209
  92.2 4.2 fusion.75
  97.5 11.0 %all_to_all.42 = bf16[8,128,128]{2,1,0:T(8,128)(2,1)S(1)} all-to-all(bf16[8,128,128]{2,1,0:T(8,128)(2,1)S(1)} %reshape.211), channel_id=1, replica_groups=mesh['ctx'=8,'fsdp'=4] {'ctx'}, dimensions={0} | all-to-all | bytes 524288 | tf_op jit(solution)/shard_map/all_to_all | solution.py:355
  113.8 3.5 all-to-all-start.1
  117.4 17.5 %all-to-all-done.1 = bf16[656,4,256]{2,0,1:T(8,128)(2,1)S(1)} async-done(((bf16[656,4,256]{2,0,1:T(8,128)(2,1)}), bf16[656,4,256]{2,0,1:T(8,128)(2,1)S(1)}, u32[]{:S(2)}, u32[]{:S(2)}) %all-to-all-start.1) | async-done | bytes 1343520 | tf_op jit(solution)/shard_map/all_to_all | solution.py:324
  134.9 7.7 all_gather.41
  142.6 17.5 %all-gather.15.cloned.1.call-done = bf16[1024,1024]{1,0:T(8,128)(2,1)} async-done(((bf16[128,1024]{1,0:T(8,128)(2,1)}), bf16[1024,1024]{1,0:T(8,128)(2,1)}) %all-gather.15.cloned.1.call-update) | async-done | bytes 2097168 | tf_op jit(solution)/shard_map/all_gather | solution.py:279
  160.1 5.2 fusion.77
  165.2 44.5 %all-gather.19.cloned.1.call-done = bf16[1024,1024]{1,0:T(8,128)(2,1)} async-done(((bf16[128,1024]{1,0:T(8,128)(2,1)}), bf16[1024,1024]{1,0:T(8,128)(2,1)}) %all-gather.19.cloned.1.call-update) | async-done | bytes 2097168 | tf_op jit(solution)/shard_map/all_gather | solution.py:279
  209.7 6.4 multiply_convert_fusion.1
  226.8 3.3 convolution_convert_fusion.6
  230.2 4.4 convolution_convert_fusion.4
  234.9 52.6 %reduce-scatter.10.cloned.1.call-done = bf16[128,1024]{1,0:T(8,128)(2,1)} async-done(((bf16[1024,1024]{1,0:T(8,128)(2,1)}), bf16[128,1024]{1,0:T(8,128)(2,1)}) %reduce-scatter.10.cloned.1.call-update) | async-done | bytes 262160 | tf_op jit(solution)/shard_map/reduce_scatter | solution.py:283
  288.7 70.5 %reduce-scatter.8.cloned.1.call-done = bf16[128,1024]{1,0:T(8,128)(2,1)} async-done(((bf16[1024,1024]{1,0:T(8,128)(2,1)}), bf16[128,1024]{1,0:T(8,128)(2,1)}) %reduce-scatter.8.cloned.1.call-update) | async-done | bytes 262160 | tf_op jit(solution)/shard_map/reduce_scatter | solution.py:283
  366.3 3.7 all-to-all-start.2
  370.8 12.6 %reduce-scatter.20.cloned.1.call-done = bf16[328,256]{1,0:T(8,128)(2,1)} async-done(((bf16[328,1024]{1,0:T(8,128)(2,1)}), bf16[328,256]{1,0:T(8,128)(2,1)}) %reduce-scatter.20.cloned.1.call-update) | async-done | bytes 167952 | tf_op jit(solution)/shard_map/reduce_scatter | solution.py:388
  388.1 3.4 multiply_convert_fusion
  398.3 3.8 convolution_convert_fusion.5
  402.2 10.4 %reduce-scatter.18.cloned.1.call-done = bf16[656,256]{1,0:T(8,128)(2,1)} async-done(((bf16[656,1024]{1,0:T(8,128)(2,1)}), bf16[656,256]{1,0:T(8,128)(2,1)}) %reduce-scatter.18.cloned.1.call-update) | async-done | bytes 335888 | tf_op jit(solution)/shard_map/reduce_scatter | solution.py:381
  415.4 31.4 %reduce-scatter.16.cloned.1.call-done = bf16[256,1024]{1,0:T(8,128)(2,1)} async-done(((bf16[1024,1024]{1,0:T(8,128)(2,1)}), bf16[256,1024]{1,0:T(8,128)(2,1)}) %reduce-scatter.16.cloned.1.call-update) | async-done | bytes 524304 | tf_op jit(solution)/shard_map/reduce_scatter | solution.py:405
  446.8 44.3 %all-gather.21.cloned.1.call-done = bf16[2624,256]{1,0:T(8,128)(2,1)} async-done(((bf16[328,256]{1,0:T(8,128)(2,1)}), bf16[2624,256]{1,0:T(8,128)(2,1)}) %all-gather.21.cloned.1.call-update) | async-done | bytes 1343504 | tf_op jit(solution)/shard_map/all_gather | solution.py:389
  491.1 4.3 all-to-all-start.3
  495.7 22.5 %reduce-scatter.14.cloned.1.call-done = bf16[256,384]{1,0:T(8,128)(2,1)} async-done(((bf16[1024,384]{1,0:T(8,128)(2,1)}), bf16[256,384]{1,0:T(8,128)(2,1)}) %reduce-scatter.14.cloned.1.call-update) | async-done | bytes 196624 | tf_op jit(solution)/shard_map/reduce_scatter | solution.py:438
  518.2 3.7 copy.87
  525.9 47.7 %all-gather.25.cloned.1.call-done = bf16[5248,256]{1,0:T(8,128)(2,1)} async-done(((bf16[656,256]{1,0:T(8,128)(2,1)}), bf16[5248,256]{1,0:T(8,128)(2,1)}) %all-gather.25.cloned.1.call-update) | async-done | bytes 2686992 | tf_op jit(solution)/shard_map/all_gather | solution.py:382
  573.6 4.5 copy.88
  578.2 6.0 copy.91
  588.0 56.5 %reduce-scatter.12.cloned.1.call-done = bf16[128,1024]{1,0:T(8,128)(2,1)} async-done(((bf16[1024,1024]{1,0:T(8,128)(2,1)}), bf16[128,1024]{1,0:T(8,128)(2,1)}) %reduce-scatter.12.cloned.1.call-update) | async-done | bytes 262160 | tf_op jit(solution)/shard_map/reduce_scatter | solution.py:283
  647.7 72.0 %all-reduce.2.cloned.1.call-done = bf16[256,1024]{1,0:T(8,128)(2,1)} async-done(((bf16[256,1024]{1,0:T(8,128)(2,1)}), bf16[256,1024]{1,0:T(8,128)(2,1)}) %all-reduce.2.cloned.1.call-update) | async-done | bytes 524304 | tf_op jit(solution)/shard_map/psum | solution.py:406
  721.8 43.3 %all-gather.23.cloned.1.call-done = bf16[2048,384]{1,0:T(8,128)(2,1)} async-done(((bf16[256,384]{1,0:T(8,128)(2,1)}), bf16[2048,384]{1,0:T(8,128)(2,1)}) %all-gather.23.cloned.1.call-update) | async-done | bytes 1572880 | tf_op jit(solution)/shard_map/all_gather | solution.py:439
  (193 shorter events, 94.0 us)
Async XLA Ops:
  7.2 3.8 copy-start.26
  7.2 3.8 copy-start.28
  7.2 3.9 copy-start.13
  7.2 54.8 %all-gather.11.cloned.1.call-start = ((), (), s32[]{:S(2)}) async-start(), calls=%async_computation.11 | async-start | bytes 2359296 | tf_op jit(solution)/shard_map/all_gather | solution.py:279
  7.9 100.8 %all-gather.13.cloned.1.call-start = ((), (), s32[]{:S(2)}) async-start(), calls=%async_computation.12 | async-start | bytes 2621440 | tf_op jit(solution)/shard_map/all_gather | solution.py:322
  8.7 133.9 %all-gather.17.cloned.1.call-start = ((), (), s32[]{:S(2)}) async-start(), calls=%async_computation.14 | async-start | bytes 1966080 | tf_op jit(solution)/shard_map/all_gather | solution.py:323
  10.9 149.2 %all-gather.15.cloned.1.call-start = ((), (), s32[]{:S(2)}) async-start(), calls=%async_computation.13 | async-start | bytes 2359296 | tf_op jit(solution)/shard_map/all_gather | solution.py:279
  11.8 52.3 %copy-start.4 = (bf16[256,3072]{0,1:T(8,128)(2,1)}, bf16[256,3072]{0,1:T(8,128)(2,1)S(1)}, u32[]{:S(2)}) copy-start(bf16[256,3072]{0,1:T(8,128)(2,1)S(1)} %copy.69) | copy-start | bytes 4718596
  22.0 43.6 %copy-start.16 = (bf16[1024,386]{0,1:T(8,128)(2,1)}, bf16[1024,386]{0,1:T(8,128)(2,1)S(1)}, u32[]{:S(2)}) copy-start(bf16[1024,386]{0,1:T(8,128)(2,1)S(1)} %all_gather.37) | copy-start | bytes 2371588
  96.7 12.0 %copy-start.2 = (bf16[2,64,1024]{2,1,0:T(8,128)(2,1)S(1)}, bf16[2,64,1024]{2,1,0:T(8,128)(2,1)}, u32[]{:S(2)}) copy-start(bf16[2,64,1024]{2,1,0:T(8,128)(2,1)} %param.8) | copy-start | bytes 786436
  112.0 97.7 %all-gather.19.cloned.1.call-start = ((), (), s32[]{:S(2)}) async-start(), calls=%async_computation.16 | async-start | bytes 2359296 | tf_op jit(solution)/shard_map/all_gather | solution.py:279
  113.8 21.1 %all-to-all-start.1 = ((bf16[656,4,256]{2,0,1:T(8,128)(2,1)}), bf16[656,4,256]{2,0,1:T(8,128)(2,1)S(1)}, u32[]{:S(2)}, u32[]{:S(2)}) async-start(bf16[656,4,256]{2,0,1:T(8,128)(2,1)} %bitcast.125), calls=%async_computation.1 | async-start | bytes 2686976 | tf_op jit(solution)/shard_map/all_to_all | solution.py:324
  117.3 170.3 %reduce-scatter.10.cloned.1.call-start = ((), (), s32[]{:S(2)}) async-start(), calls=%async_computation.17 | async-start | bytes 2359296 | tf_op jit(solution)/shard_map/reduce_scatter | solution.py:283
  209.7 7.6 copy-start.30
  220.5 138.8 %reduce-scatter.8.cloned.1.call-start = ((), (), s32[]{:S(2)}) async-start(), calls=%async_computation.15 | async-start | bytes 2359296 | tf_op jit(solution)/shard_map/reduce_scatter | solution.py:283
  225.6 4.5 copy-start.32
  225.6 157.8 %reduce-scatter.20.cloned.1.call-start = ((), (), s32[]{:S(2)}) async-start(), calls=%async_computation.23 | async-start | bytes 839680 | tf_op jit(solution)/shard_map/reduce_scatter | solution.py:388
  230.1 182.5 %reduce-scatter.18.cloned.1.call-start = ((), (), s32[]{:S(2)}) async-start(), calls=%async_computation.22 | async-start | bytes 1679360 | tf_op jit(solution)/shard_map/reduce_scatter | solution.py:381
  234.6 124.7 %copy-start.15 = (bf16[2,64,1024]{2,1,0:T(8,128)(2,1)S(1)}, bf16[2,64,1024]{2,1,0:T(8,128)(2,1)}, u32[]{:S(2)}) copy-start(bf16[2,64,1024]{2,1,0:T(8,128)(2,1)} %param.15) | copy-start | bytes 786436
  234.6 212.1 %reduce-scatter.16.cloned.1.call-start = ((), (), s32[]{:S(2)}) async-start(), calls=%async_computation.20 | async-start | bytes 2621440 | tf_op jit(solution)/shard_map/reduce_scatter | solution.py:405
  366.3 17.1 %all-to-all-start.2 = ((bf16[8,128,128]{2,1,0:T(8,128)(2,1)}), bf16[8,128,128]{2,1,0:T(8,128)(2,1)S(1)}, u32[]{:S(2)}, u32[]{:S(2)}) async-start(bf16[8,128,128]{2,1,0:T(8,128)(2,1)} %bitcast.127), calls=%async_computation.4 | async-start | bytes 524288 | tf_op jit(solution)/shard_map/all_to_all | solution.py:399
  370.0 121.1 %all-gather.21.cloned.1.call-start = ((), (), s32[]{:S(2)}) async-start(), calls=%async_computation.24 | async-start | bytes 1511424 | tf_op jit(solution)/shard_map/all_gather | solution.py:389
  383.4 134.8 %reduce-scatter.14.cloned.1.call-start = ((), (), s32[]{:S(2)}) async-start(), calls=%async_computation.19 | async-start | bytes 983040 | tf_op jit(solution)/shard_map/reduce_scatter | solution.py:438
  384.6 3.1 copy-start.23
  388.1 3.4 copy-start.11
  398.3 14.4 %copy-start.17 = (bf16[1024,386]{0,1:T(8,128)(2,1)S(1)}, bf16[1024,386]{0,1:T(8,128)(2,1)}, u32[]{:S(2)}) copy-start(bf16[1024,386]{0,1:T(8,128)(2,1)} %copy-done.16) | copy-start | bytes 2371588
  402.1 171.5 %all-gather.25.cloned.1.call-start = ((), (), s32[]{:S(2)}) async-start(), calls=%async_computation.26 | async-start | bytes 3022848 | tf_op jit(solution)/shard_map/all_gather | solution.py:382
  412.7 231.9 %reduce-scatter.12.cloned.1.call-start = ((), (), s32[]{:S(2)}) async-start(), calls=%async_computation.18 | async-start | bytes 2359296 | tf_op jit(solution)/shard_map/reduce_scatter | solution.py:283
  415.3 304.4 %all-reduce.2.cloned.1.call-start = ((), (), s32[]{:S(2)}) async-start(), calls=%async_computation.21 | async-start | bytes 1048576 | tf_op jit(solution)/shard_map/psum | solution.py:406
  491.1 31.4 %all-to-all-start.3 = ((bf16[4,656,256]{2,1,0:T(8,128)(2,1)}), bf16[4,656,256]{2,1,0:T(8,128)(2,1)}, u32[]{:S(2)}, u32[]{:S(2)}) async-start(bf16[4,656,256]{2,1,0:T(8,128)(2,1)} %bitcast.145), calls=%async_computation.10 | async-start | bytes 2686976 | tf_op jit(solution)/shard_map/all_to_all | solution.py:390
  495.4 269.7 %all-gather.23.cloned.1.call-start = ((), (), s32[]{:S(2)}) async-start(), calls=%async_computation.25 | async-start | bytes 1769472 | tf_op jit(solution)/shard_map/all_gather | solution.py:439
  584.2 3.3 copy-start.27
  (21 other events, 28.7 us)
Sparse Core Ops, SparseCore 0:
  10.1 51.7 all-gather.10
  63.5 21.0 all-gather.12
  86.2 19.6 all-gather.16
  112.1 47.9 all-gather.14
  162.1 47.6 all-gather.18
  220.6 66.8 reduce-scatter.9
  291.7 67.5 reduce-scatter.7
  361.8 21.5 reduce-scatter.19
  386.0 26.6 reduce-scatter.17
  415.6 31.1 reduce-scatter.15
  449.0 42.0 all-gather.20
  494.0 24.1 reduce-scatter.13
  520.4 53.2 all-gather.24
  577.6 66.8 reduce-scatter.11
  647.8 71.8 all-reduce.1
  721.7 43.3 all-gather.22

commit v2 on v1

--- a/solution.py
+++ b/solution.py
@@ -275,14 +275,55 @@
     )
 
 
+def ring_order(blocks):
+    return list(range(0, blocks, 2)) + list(range(blocks - 1, 0, -2))
+
+
+def ring_moves(blocks):
+    order = ring_order(blocks)
+    ahead = [(order[i], order[(i + 1) % blocks]) for i in range(blocks)]
+    return ahead, [(after, before) for before, after in ahead]
+
+
 def gather_tokens(rows):
-    return lax.all_gather(rows, "ctx", axis=0, tiled=True)
+    blocks = lax.axis_size("ctx")
+    half, cut = blocks // 2, rows.shape[0] // 2
+    ahead, behind = ring_moves(blocks)
+    found = [rows] + [None] * (blocks - 1)
+    from_before = from_after = rows
+    for step in range(1, half):
+        from_before = lax.ppermute(from_before, "ctx", ahead)
+        from_after = lax.ppermute(from_after, "ctx", behind)
+        found[blocks - step] = from_before
+        found[step] = from_after
+    found[half] = jnp.concatenate(
+        [
+            lax.ppermute(from_before[:cut], "ctx", ahead),
+            lax.ppermute(from_after[cut:], "ctx", behind),
+        ]
+    )
+    return jnp.concatenate(found)
 
 
 def scatter_tokens(partial_rows):
-    return lax.psum_scatter(
-        partial_rows.astype(jnp.bfloat16), "ctx", scatter_dimension=0, tiled=True
-    ).astype(jnp.float32)
+    blocks = lax.axis_size("ctx")
+    half = blocks // 2
+    rows = partial_rows.shape[0] // blocks
+    cut = rows // 2
+    ahead, behind = ring_moves(blocks)
+    terms = [partial_rows[i * rows : (i + 1) * rows] for i in range(blocks)]
+    to_ahead = lax.ppermute(terms[half][:cut].astype(jnp.bfloat16), "ctx", ahead)
+    to_behind = lax.ppermute(terms[half][cut:].astype(jnp.bfloat16), "ctx", behind)
+    for step in range(half - 1, 0, -1):
+        to_ahead, to_behind = to_ahead.astype(jnp.float32), to_behind.astype(jnp.float32)
+        if step == half - 1:
+            to_ahead = jnp.concatenate([to_ahead, jnp.zeros_like(to_ahead)])
+            to_behind = jnp.concatenate([jnp.zeros_like(to_behind), to_behind])
+        to_ahead = (terms[step] + to_ahead).astype(jnp.bfloat16)
+        to_behind = (terms[blocks - step] + to_behind).astype(jnp.bfloat16)
+        to_ahead = lax.ppermute(to_ahead, "ctx", ahead)
+        to_behind = lax.ppermute(to_behind, "ctx", behind)
+    return terms[0] + to_ahead.astype(jnp.float32) + to_behind.astype(jnp.float32)
 
 
 def by_heads(inputs, gain_one, w_qkv, w_attn, gain_two, w_in, w_ffn, cotangent):
@@ -300,6 +341,12 @@
     scale_factor = HEAD_DIM ** (-0.5)
     f32, bf16 = jnp.float32, jnp.bfloat16
 
+    order = ring_order(blocks)
+    places = jnp.array([order.index(i) for i in range(blocks)], jnp.int32)
+    place = places[block]
+    ring_block = jnp.array(order, jnp.int32)[(place + jnp.arange(blocks)) % blocks]
+    positions = ring_block[:, None] * tok_seq + jnp.arange(tok_seq, dtype=jnp.int32)[None, :]
+
     own_x = inputs.reshape(own_rows, D)
     own_cot = cotangent.reshape(own_rows, D)
 
@@ -333,7 +380,7 @@
     normed_all, _ = norm_parts(all_x.astype(f32))
     input_one = (normed_all * full_g1).astype(bf16)
     project = jnp.dot(input_one, qkv_c, preferred_element_type=f32)
-    cosine, sine_part = rotary_tables(jnp.arange(seq_len, dtype=jnp.int32))
+    cosine, sine_part = rotary_tables(positions.reshape(seq_len))
     shaped = project.reshape(blocks, seq_dev, tok_seq, 3, heads_dev, HEAD_DIM)
     shaped = shaped.transpose(3, 1, 0, 2, 4, 5).reshape(3, seq_dev, seq_len, heads_dev, HEAD_DIM)
     queries = rotate(shaped[0], cosine, sine_part).astype(bf16)
@@ -352,7 +399,8 @@
     log_sum = row_max + jnp.log(row_sum)
     attn_b = attn_f.astype(bf16).reshape(seq_dev, heads_dev, blocks, tok_seq, HEAD_DIM)
     attn_b = attn_b.transpose(2, 0, 3, 1, 4).reshape(blocks, own_rows, head_cols)
-    own_attn = lax.all_to_all(attn_b, "ctx", split_axis=0, concat_axis=0, tiled=True)
+    by_block = jnp.take(attn_b, (places - place) % blocks, axis=0)
+    own_attn = lax.all_to_all(by_block, "ctx", split_axis=0, concat_axis=0, tiled=True)
     own_attn = own_attn.transpose(1, 0, 2).reshape(own_rows, D)
 
     resid = own_x.astype(f32) + jnp.dot(own_attn, full_attn, preferred_element_type=f32)
@@ -392,18 +440,19 @@
 
     own_resid = own_cot.astype(f32) + norm_back(own_grad_two * full_g2, normed_two, inv_two)
     resid_b = own_resid.astype(bf16)
-    own_mixed = lax.dot_general(
-        resid_b, full_attn, (((1,), (1,)), ((), ())), preferred_element_type=f32
-    ).astype(bf16)
-    own_mixed = own_mixed.reshape(own_rows, blocks, head_cols).transpose(1, 0, 2)
-    mixed = lax.all_to_all(own_mixed, "ctx", split_axis=0, concat_axis=0, tiled=True)
+    all_resid = gather_tokens(resid_b)
+    attn_c = lax.dynamic_slice_in_dim(full_attn, block * head_cols, head_cols, 0)
+    mixed = lax.dot_general(
+        all_resid, attn_c, (((1,), (1,)), ((), ())), preferred_element_type=f32
+    ).astype(bf16)
     mixed = mixed.reshape(blocks, seq_dev, tok_seq, heads_dev, HEAD_DIM).transpose(1, 3, 0, 2, 4)
     mixed = mixed.reshape(seq_dev, heads_dev, seq_len, HEAD_DIM)
     grad_attn = lax.dot_general(
-        own_attn, resid_b, (((0,), (0,)), ((), ())), preferred_element_type=f32
-    ).astype(bf16)
-    grad_attn = lax.psum_scatter(grad_attn, "fsdp", scatter_dimension=0, tiled=True)
-    grad_attn = lax.psum(grad_attn, "ctx").astype(f32)
+        attn_b.reshape(all_rows, head_cols),
+        all_resid,
+        (((0,), (0,)), ((), ())),
+        preferred_element_type=f32,
+    ).astype(bf16)
 
     row_delta = jnp.sum(mixed.astype(f32) * attn_f, axis=-1, keepdims=True)
     probs = jnp.exp(scores - log_sum)
@@ -433,12 +482,16 @@
         lax.dot_general(joint, qkv_c, (((1,), (1,)), ((), ())), preferred_element_type=f32)
     )
     grad_qkv = lax.dot_general(
-        input_one, joint, (((0,), (0,)), ((), ())), preferred_element_type=f32
-    ).astype(bf16)
-    grad_qkv = lax.psum_scatter(grad_qkv, "fsdp", scatter_dimension=0, tiled=True)
-    grad_qkv = lax.all_gather(grad_qkv, "ctx", axis=0, tiled=False)
-    grad_qkv = grad_qkv.reshape(blocks, row_part, 3, head_cols).transpose(1, 2, 0, 3)
-    grad_qkv = grad_qkv.reshape(row_part, 3 * D).astype(f32)
+        joint, input_one, (((0,), (0,)), ((), ())), preferred_element_type=f32
+    ).astype(bf16)
+    grads = jnp.concatenate([grad_qkv, grad_attn])
+    grads = lax.psum_scatter(grads, "fsdp", scatter_dimension=1, tiled=True)
+    grads = lax.all_gather(grads, "ctx", axis=0, tiled=False)
+    grad_qkv = grads[:, : 3 * head_cols].reshape(blocks, 3, head_cols, row_part)
+    grad_qkv = grad_qkv.transpose(1, 0, 2, 3).reshape(3 * D, row_part).T.astype(f32)
+    grad_attn = grads[:, 3 * head_cols :].reshape(D, row_part)
+    grad_attn = lax.all_to_all(grad_attn, "fsdp", split_axis=0, concat_axis=1, tiled=True)
+    grad_attn = grad_attn.astype(f32)
     normed_one, inv_one = norm_parts(own_x.astype(f32))
     grad_input = own_resid + norm_back(own_grad_one * full_g1, normed_one, inv_one)
 
@@ -458,7 +511,7 @@
 
 def solution(mesh):
     blocks = mesh.shape["ctx"]
-    split_ok = HEADS % blocks == 0 and FF % blocks == 0 and (D // blocks) % 128 == 0
+    split_ok = blocks % 4 == 0 and HEADS % blocks == 0 and FF % blocks == 0 and (D // blocks) % 128 == 0
 
     return jax.shard_map(
         by_heads if split_ok else on_device,

time: 790 us -> 503 us (0.64)
  waiting for transfers between devices: 584 us -> 214 us
  starting transfers between devices: 12.6 us -> 81.5 us
  local copies, waits for them, and re-layouts: 58.1 us -> 86.1 us
  matrix products: 51.6 us -> 40.6 us
  other arithmetic: 29.5 us -> 39.1 us
    reduce_scatter x5 -> x1, waiting for transfers between devices: 234 us -> 8.76 us  [by_heads(): grads = lax.psum_scatter(grads, 'fsdp', scatter_dimension=1, tiled=True)]
    all_gather x4 -> x1, waiting for transfers between devices: 144 us -> 35.4 us  [by_heads(): grads = lax.all_gather(grads, 'ctx', axis=0, tiled=False)]
    ppermute x0 -> x56, waiting for transfers between devices: none -> 101 us  [the longest x9 32.6 us: scatter_tokens(): to_behind = lax.ppermute(to_behind, 'ctx', behind)]
    psum x1 -> x0, waiting for transfers between devices: 72 us -> none  [by_heads(): grad_attn = lax.psum(grad_attn, 'ctx').astype(f32)]
    ppermute x0 -> x56, starting transfers between devices: none -> 63.1 us  [the longest x12 18.2 us: gather_tokens(): from_after = lax.ppermute(from_after, 'ctx', behind)]
    all_gather x1, waiting for transfers between devices: 44.3 us -> 21.5 us  [by_heads(): grad_ffn = lax.all_gather(grad_ffn, 'ctx', axis=0, tiled=True)]
    all_gather x1, waiting for transfers between devices: 47.7 us -> 29.8 us  [by_heads(): grad_in = lax.all_gather(grad_in, 'ctx', axis=0, tiled=False)]
    all_to_all x1, waiting for transfers between devices: 17.5 us -> 0.39 us  [by_heads(): lax.all_to_all(w_ffn, 'fsdp', split_axis=1, concat_axis=0, tiled=True)]
  transfers between devices with their start and end apart: 19 -> 68, of which waited for: 15 -> 40; matrix products, arithmetic and copies ran while one was open for 15% -> 28% of each run, Pallas kernels for 0% -> 0%
where the time goes in v2:
time: 503 us; the launch traced here: 498 us
  waiting for transfers between devices  214 us (43%)
  local copies, waits for them, and re-layouts  86.1 us (17%)
  starting transfers between devices  81.5 us (16%)
  matrix products  40.6 us (8%)
  other arithmetic  39.1 us (8%)
  blocking collectives  21.2 us (4%)
  between operations  15.5 us (3%)
    unnamed x120, local copies, waits for them, and re-layouts  37.8 us
    all_gather x1, waiting for transfers between devices, by_heads(): grads = lax.all_gather(grads, 'ctx', axis=0, tiled=False)  35.4 us
    ppermute x9, waiting for transfers between devices, scatter_tokens(): to_behind = lax.ppermute(to_behind, 'ctx', behind)  32.6 us
    all_gather x1, waiting for transfers between devices, by_heads(): grad_in = lax.all_gather(grad_in, 'ctx', axis=0, tiled=False)  29.8 us
    all_gather x1, waiting for transfers between devices, by_heads(): grad_ffn = lax.all_gather(grad_ffn, 'ctx', axis=0, tiled=True)  21.5 us
    ppermute x9, waiting for transfers between devices, scatter_tokens(): to_ahead = lax.ppermute(to_ahead, 'ctx', ahead)  19.1 us
    ppermute x12, starting transfers between devices, gather_tokens(): from_after = lax.ppermute(from_after, 'ctx', behind)  18.2 us
    ppermute x12, waiting for transfers between devices, gather_tokens(): from_before = lax.ppermute(from_before, 'ctx', ahead)  16.3 us
  transfers between devices with their start and end apart: 68, of which 40 were waited for; matrix products, arithmetic and copies ran while one was open for 28% of the time, Pallas kernels for 0%

profile of v2, /device:TPU:0, one launch (start us, length us, event | category | flops | bytes accessed | tf_op | source)
XLA Modules:
  0.0 498.3 jit_solution(1567926020576542766)
XLA Ops:
  18.0 13.3 %all_gather.27 = bf16[1024,386]{0,1:T(8,128)(2,1)S(1)} all-gather(bf16[256,386]{0,1:T(8,128)(2,1)S(1)} %pad_maximum_fusion.5), channel_id=1, replica_groups=mesh['ctx'=8,'fsdp'=4] {'fsdp'}, dimensions={0}, use_global_device_ids=true | all-gather | bytes 988160 | tf_op jit(solution)/shard_map/all_gather | solution.py:364
  37.9 6.0 %collective-permute-done.4 = bf16[128,1024]{1,0:T(8,128)(2,1)S(1)} collective-permute-done((bf16[128,1024]{1,0:T(8,128)(2,1)S(1)}, bf16[128,1024]{1,0:T(8,128)(2,1)S(1)}, u32[]{:S(2)}, u32[]{:S(2)}) %collective-permute-start.4) | collective-permute-done | bytes 262176 | tf_op jit(solution)/shard_map/ppermute | solution.py:295
  48.1 5.0 %collective-permute-done.5 = bf16[128,1024]{1,0:T(8,128)(2,1)S(1)} collective-permute-done((bf16[128,1024]{1,0:T(8,128)(2,1)S(1)}, bf16[128,1024]{1,0:T(8,128)(2,1)S(1)}, u32[]{:S(2)}, u32[]{:S(2)}) %collective-permute-start.5) | collective-permute-done | bytes 262176 | tf_op jit(solution)/shard_map/ppermute | solution.py:295
  61.3 4.4 collective-permute-done.7
  91.1 5.9 %all-to-all-start = ((bf16[8,128,128]{2,1,0:T(8,128)(2,1)}), bf16[8,128,128]{2,1,0:T(8,128)(2,1)S(1)}, u32[]{:S(2)}, u32[]{:S(2)}) async-start(bf16[8,128,128]{2,1,0:T(8,128)(2,1)} %broadcast_select_fusion), calls=%async_computation | async-start | bytes 524288 | tf_op jit(solution)/shard_map/all_to_all | solution.py:403
  108.2 3.5 all-to-all-start.1
  134.6 7.8 %all_gather.30 = bf16[328,1024]{1,0:T(8,128)(2,1)S(1)} all-gather(bf16[328,256]{1,0:T(8,128)(2,1)S(1)} %constant_dynamic-slice_fusion), channel_id=1, replica_groups=mesh['ctx'=8,'fsdp'=4] {'fsdp'}, dimensions={1}, use_global_device_ids=true | all-gather | bytes 839680 | tf_op jit(solution)/shard_map/all_gather | solution.py:372
  157.6 3.7 fusion.114
  161.3 5.6 %multiply_convert_fusion.1 = (bf16[1024,328]{0,1:T(8,128)(2,1)S(1)}, f32[1024,328]{0,1:T(8,128)S(1)}, bf16[1024,328]{0,1:T(8,128)(2,1)S(1)}) fusion(f32[1024,656]{0,1:T(8,128)S(1)} %fusion.114, bf16[1024,1024]{1,0:T(8,128)(2,1)} %constant_dynamic-update-slice_fusion.18, bf16[328,1024]{1,0:T(8,128)(2,1)S(1)} %all_gather.30), kind=kOutput, calls=%fused_computation.42 | convolution fusion | flops 713728000 | bytes 8142848 | tf_op jit(solution)/shard_map/dot_general | solution.py:415
  180.0 4.0 collective-permute-done.33
  191.2 4.0 collective-permute-done.34
  199.9 3.4 collective-permute-done.37
  205.4 3.5 collective-permute-done.21
  210.3 4.3 collective-permute-done.38
  234.0 4.9 collective-permute-done.40
  248.4 4.6 convolution_convert_fusion
  272.1 3.4 multiply_convert_fusion
  301.1 5.1 %collective-permute-done.49 = bf16[128,1024]{1,0:T(8,128)(2,1)S(1)} collective-permute-done((bf16[128,1024]{1,0:T(8,128)(2,1)S(1)}, bf16[128,1024]{1,0:T(8,128)(2,1)S(1)}, u32[]{:S(2)}, u32[]{:S(2)}) %collective-permute-start.49) | collective-permute-done | bytes 262176 | tf_op jit(solution)/shard_map/ppermute | solution.py:324
  308.3 8.8 %reduce-scatter.4.cloned.1.call-done = bf16[512,256]{1,0:T(8,128)(2,1)} async-done(((bf16[512,1024]{1,0:T(8,128)(2,1)}), bf16[512,256]{1,0:T(8,128)(2,1)}) %reduce-scatter.4.cloned.1.call-update) | async-done | bytes 262160 | tf_op jit(solution)/shard_map/reduce_scatter | solution.py:488
  320.0 6.4 %collective-permute-done.53 = bf16[128,1024]{1,0:T(8,128)(2,1)S(1)} collective-permute-done((bf16[128,1024]{1,0:T(8,128)(2,1)S(1)}, bf16[128,1024]{1,0:T(8,128)(2,1)S(1)}, u32[]{:S(2)}, u32[]{:S(2)}) %collective-permute-start.53) | collective-permute-done | bytes 262176 | tf_op jit(solution)/shard_map/ppermute | solution.py:325
  329.8 8.9 %collective-permute-done.54 = bf16[128,1024]{1,0:T(8,128)(2,1)S(1)} collective-permute-done((bf16[128,1024]{1,0:T(8,128)(2,1)S(1)}, bf16[128,1024]{1,0:T(8,128)(2,1)S(1)}, u32[]{:S(2)}, u32[]{:S(2)}) %collective-permute-start.54) | collective-permute-done | bytes 262176 | tf_op jit(solution)/shard_map/ppermute | solution.py:325
  342.4 21.5 %all-gather.12.cloned.1.call-done = bf16[2624,256]{1,0:T(8,128)(2,1)} async-done(((bf16[328,256]{1,0:T(8,128)(2,1)}), bf16[2624,256]{1,0:T(8,128)(2,1)}) %all-gather.12.cloned.1.call-update) | async-done | bytes 1343504 | tf_op jit(solution)/shard_map/all_gather | solution.py:437
  363.9 4.5 all-to-all-start.3
  368.4 3.7 copy.105
  374.9 11.1 %all-to-all-done.3 = bf16[4,656,256]{2,1,0:T(8,128)(2,1)} async-done(((bf16[4,656,256]{2,1,0:T(8,128)(2,1)}), bf16[4,656,256]{2,1,0:T(8,128)(2,1)}, u32[]{:S(2)}, u32[]{:S(2)}) %all-to-all-start.3) | async-done | bytes 1343520 | tf_op jit(solution)/shard_map/all_to_all | solution.py:438
  389.5 29.8 %all-gather.16.cloned.1.call-done = bf16[5248,256]{1,0:T(8,128)(2,1)} async-done(((bf16[656,256]{1,0:T(8,128)(2,1)}), bf16[5248,256]{1,0:T(8,128)(2,1)}) %all-gather.16.cloned.1.call-update) | async-done | bytes 2686992 | tf_op jit(solution)/shard_map/all_gather | solution.py:430
  419.3 4.6 copy.106
  423.8 6.1 %copy.109 = f32[256,5248]{1,0:T(8,128)} copy(f32[256,5248]{0,1:T(8,128)} %bitcast.133) | data formatting | bytes 10747904
  433.8 35.4 %all-gather.14.cloned.1.call-done = bf16[4096,256]{1,0:T(8,128)(2,1)} async-done(((bf16[512,256]{1,0:T(8,128)(2,1)}), bf16[4096,256]{1,0:T(8,128)(2,1)}) %all-gather.14.cloned.1.call-update) | async-done | bytes 2097168 | tf_op jit(solution)/shard_map/all_gather | solution.py:489
  475.6 4.1 all-to-all-start.2
  479.8 3.7 multiply_reduce_fusion.2
  484.0 4.6 all-to-all-done.2
  (373 shorter events, 237.2 us)
Async XLA Ops:
  7.2 104.8 %all-gather.8.cloned.1.call-start = ((), (), s32[]{:S(2)}) async-start(), calls=%async_computation.7 | async-start | bytes 2621440 | tf_op jit(solution)/shard_map/all_gather | solution.py:369
  7.9 149.6 %all-gather.10.cloned.1.call-start = ((), (), s32[]{:S(2)}) async-start(), calls=%async_computation.8 | async-start | bytes 1966080 | tf_op jit(solution)/shard_map/all_gather | solution.py:370
  8.0 25.9 %collective-permute-start = (bf16[128,1024]{1,0:T(8,128)(2,1)}, bf16[128,1024]{1,0:T(8,128)(2,1)S(1)}, u32[]{:S(2)}, u32[]{:S(2)}) collective-permute-start(bf16[128,1024]{1,0:T(8,128)(2,1)} %bitcast.137), channel_id=1, source_target_pairs={{8,0},{16,8},{24,16},{28,24},{20,28},{12,20},{4,12},{0,4},{9,1},{1... | collective-permute-start | bytes 786440 | tf_op jit(solution)/shard_map/ppermute | solution.py:296
  11.0 24.6 %collective-permute-start.3 = (bf16[128,1024]{1,0:T(8,128)(2,1)}, bf16[128,1024]{1,0:T(8,128)(2,1)S(1)}, u32[]{:S(2)}, u32[]{:S(2)}) collective-permute-start(bf16[128,1024]{1,0:T(8,128)(2,1)} %bitcast.138), channel_id=1, source_target_pairs={{0,8},{8,16},{16,24},{24,28},{28,20},{20,12},{12,4},{4,0},{1,9},{9... | collective-permute-start | bytes 786440 | tf_op jit(solution)/shard_map/ppermute | solution.py:295
  11.2 33.2 %collective-permute-start.24 = (bf16[128,1024]{1,0:T(8,128)(2,1)}, bf16[128,1024]{1,0:T(8,128)(2,1)S(1)}, u32[]{:S(2)}, u32[]{:S(2)}) collective-permute-start(bf16[128,1024]{1,0:T(8,128)(2,1)} %bitcast.158), channel_id=1, source_target_pairs={{8,0},{16,8},{24,16},{28,24},{20,28},{12,20},{4,12},{0,4},{9,1},{1... | collective-permute-start | bytes 786440 | tf_op jit(solution)/shard_map/ppermute | solution.py:296
  13.0 33.0 %collective-permute-start.27 = (bf16[128,1024]{1,0:T(8,128)(2,1)}, bf16[128,1024]{1,0:T(8,128)(2,1)S(1)}, u32[]{:S(2)}, u32[]{:S(2)}) collective-permute-start(bf16[128,1024]{1,0:T(8,128)(2,1)} %bitcast.159), channel_id=1, source_target_pairs={{0,8},{8,16},{16,24},{24,28},{28,20},{20,12},{12,4},{4,0},{1,9},{9... | collective-permute-start | bytes 786440 | tf_op jit(solution)/shard_map/ppermute | solution.py:295
  33.9 12.6 %collective-permute-start.1 = (bf16[128,1024]{1,0:T(8,128)(2,1)S(1)}, bf16[128,1024]{1,0:T(8,128)(2,1)S(1)}, u32[]{:S(2)}, u32[]{:S(2)}) collective-permute-start(bf16[128,1024]{1,0:T(8,128)(2,1)S(1)} %collective-permute-done), channel_id=1, source_target_pairs={{8,0},{16,8},{24,16},{28,24},{20,28},{12,20},{4,12},{0,4},{9,1},{1... | collective-permute-start | bytes 786440 | tf_op jit(solution)/shard_map/ppermute | solution.py:296
  46.0 12.6 %collective-permute-start.28 = (bf16[128,1024]{1,0:T(8,128)(2,1)S(1)}, bf16[128,1024]{1,0:T(8,128)(2,1)}, u32[]{:S(2)}, u32[]{:S(2)}) collective-permute-start(bf16[128,1024]{1,0:T(8,128)(2,1)S(1)} %collective-permute-done.27), channel_id=1, source_target_pairs={{0,8},{8,16},{16,24},{24,28},{28,20},{20,12},{12,4},{4,0},{1,9},{9... | collective-permute-start | bytes 786440 | tf_op jit(solution)/shard_map/ppermute | solution.py:295
  46.5 12.8 %collective-permute-start.2 = (bf16[128,1024]{1,0:T(8,128)(2,1)S(1)}, bf16[128,1024]{1,0:T(8,128)(2,1)S(1)}, u32[]{:S(2)}, u32[]{:S(2)}) collective-permute-start(bf16[128,1024]{1,0:T(8,128)(2,1)S(1)} %collective-permute-done.1), channel_id=1, source_target_pairs={{8,0},{16,8},{24,16},{28,24},{20,28},{12,20},{4,12},{0,4},{9,1},{1... | collective-permute-start | bytes 786440 | tf_op jit(solution)/shard_map/ppermute | solution.py:296
  53.7 51.2 %collective-permute-start.26 = (bf16[128,1024]{1,0:T(8,128)(2,1)}, bf16[128,1024]{1,0:T(8,128)(2,1)}, u32[]{:S(2)}, u32[]{:S(2)}) collective-permute-start(bf16[128,1024]{1,0:T(8,128)(2,1)} %collective-permute-done.25), channel_id=1, source_target_pairs={{8,0},{16,8},{24,16},{28,24},{20,28},{12,20},{4,12},{0,4},{9,1},{1... | collective-permute-start | bytes 786440 | tf_op jit(solution)/shard_map/ppermute | solution.py:296
  58.6 42.7 %collective-permute-start.29 = (bf16[128,1024]{1,0:T(8,128)(2,1)}, bf16[128,1024]{1,0:T(8,128)(2,1)}, u32[]{:S(2)}, u32[]{:S(2)}) collective-permute-start(bf16[128,1024]{1,0:T(8,128)(2,1)} %collective-permute-done.28), channel_id=1, source_target_pairs={{0,8},{8,16},{16,24},{24,28},{28,20},{20,12},{12,4},{4,0},{1,9},{9... | collective-permute-start | bytes 786440 | tf_op jit(solution)/shard_map/ppermute | solution.py:295
  91.1 17.0 %all-to-all-start = ((bf16[8,128,128]{2,1,0:T(8,128)(2,1)}), bf16[8,128,128]{2,1,0:T(8,128)(2,1)S(1)}, u32[]{:S(2)}, u32[]{:S(2)}) async-start(bf16[8,128,128]{2,1,0:T(8,128)(2,1)} %broadcast_select_fusion), calls=%async_computation | async-start | bytes 524288 | tf_op jit(solution)/shard_map/all_to_all | solution.py:403
  102.9 14.4 %collective-permute-start.30 = (bf16[64,1024]{1,0:T(8,128)(2,1)}, bf16[64,1024]{1,0:T(8,128)(2,1)S(1)}, u32[]{:S(2)}, u32[]{:S(2)}) collective-permute-start(bf16[64,1024]{1,0:T(8,128)(2,1)} %slice.260), channel_id=1, source_target_pairs={{0,8},{8,16},{16,24},{24,28},{28,20},{20,12},{12,4},{4,0},{1,9},{9... | collective-permute-start | bytes 393224 | tf_op jit(solution)/shard_map/ppermute | solution.py:301
  106.5 11.4 %collective-permute-start.31 = (bf16[64,1024]{1,0:T(8,128)(2,1)}, bf16[64,1024]{1,0:T(8,128)(2,1)}, u32[]{:S(2)}, u32[]{:S(2)}) collective-permute-start(bf16[64,1024]{1,0:T(8,128)(2,1)} %slice.261), channel_id=1, source_target_pairs={{8,0},{16,8},{24,16},{28,24},{20,28},{12,20},{4,12},{0,4},{9,1},{1... | collective-permute-start | bytes 393224 | tf_op jit(solution)/shard_map/ppermute | solution.py:302
  108.2 21.1 %all-to-all-start.1 = ((bf16[656,4,256]{2,0,1:T(8,128)(2,1)}), bf16[656,4,256]{2,0,1:T(8,128)(2,1)S(1)}, u32[]{:S(2)}, u32[]{:S(2)}) async-start(bf16[656,4,256]{2,0,1:T(8,128)(2,1)} %bitcast.132), calls=%async_computation.1 | async-start | bytes 2686976 | tf_op jit(solution)/shard_map/all_to_all | solution.py:371
  111.7 179.7 %reduce-scatter.8.cloned.1.call-start = ((), (), s32[]{:S(2)}) async-start(), calls=%async_computation.11 | async-start | bytes 839680 | tf_op jit(solution)/shard_map/reduce_scatter | solution.py:436
  132.6 14.7 %collective-permute-start.10 = (bf16[128,1024]{1,0:T(8,128)(2,1)}, bf16[128,1024]{1,0:T(8,128)(2,1)S(1)}, u32[]{:S(2)}, u32[]{:S(2)}) collective-permute-start(bf16[128,1024]{1,0:T(8,128)(2,1)} %collective-permute-done.9), channel_id=1, source_target_pairs={{8,0},{16,8},{24,16},{28,24},{20,28},{12,20},{4,12},{0,4},{9,1},{1... | collective-permute-start | bytes 786440 | tf_op jit(solution)/shard_map/ppermute | solution.py:296
  178.4 11.2 %collective-permute-start.17 = (bf16[128,1024]{1,0:T(8,128)(2,1)S(1)}, bf16[128,1024]{1,0:T(8,128)(2,1)S(1)}, u32[]{:S(2)}, u32[]{:S(2)}) collective-permute-start(bf16[128,1024]{1,0:T(8,128)(2,1)S(1)} %fusion.77), channel_id=1, source_target_pairs={{0,8},{8,16},{16,24},{24,28},{28,20},{20,12},{12,4},{4,0},{1,9},{9... | collective-permute-start | bytes 786440 | tf_op jit(solution)/shard_map/ppermute | solution.py:324
  184.1 11.2 %collective-permute-start.34 = (bf16[128,1024]{1,0:T(8,128)(2,1)S(1)}, bf16[128,1024]{1,0:T(8,128)(2,1)S(1)}, u32[]{:S(2)}, u32[]{:S(2)}) collective-permute-start(bf16[128,1024]{1,0:T(8,128)(2,1)S(1)} %fusion.70), channel_id=1, source_target_pairs={{0,8},{8,16},{16,24},{24,28},{28,20},{20,12},{12,4},{4,0},{1,9},{9... | collective-permute-start | bytes 786440 | tf_op jit(solution)/shard_map/ppermute | solution.py:324
  203.4 11.2 %collective-permute-start.38 = (bf16[128,1024]{1,0:T(8,128)(2,1)S(1)}, bf16[128,1024]{1,0:T(8,128)(2,1)S(1)}, u32[]{:S(2)}, u32[]{:S(2)}) collective-permute-start(bf16[128,1024]{1,0:T(8,128)(2,1)S(1)} %fusion.67), channel_id=1, source_target_pairs={{8,0},{16,8},{24,16},{28,24},{20,28},{12,20},{4,12},{0,4},{9,1},{1... | collective-permute-start | bytes 786440 | tf_op jit(solution)/shard_map/ppermute | solution.py:325
  204.0 18.4 %collective-permute-start.35 = (bf16[128,1024]{1,0:T(8,128)(2,1)S(1)}, bf16[128,1024]{1,0:T(8,128)(2,1)S(1)}, u32[]{:S(2)}, u32[]{:S(2)}) collective-permute-start(bf16[128,1024]{1,0:T(8,128)(2,1)S(1)} %get-tuple-element.58), channel_id=1, source_target_pairs={{0,8},{8,16},{16,24},{24,28},{28,20},{20,12},{12,4},{4,0},{1,9},{9... | collective-permute-start | bytes 786440 | tf_op jit(solution)/shard_map/ppermute | solution.py:324
  214.6 11.2 %collective-permute-start.39 = (bf16[128,1024]{1,0:T(8,128)(2,1)S(1)}, bf16[128,1024]{1,0:T(8,128)(2,1)S(1)}, u32[]{:S(2)}, u32[]{:S(2)}) collective-permute-start(bf16[128,1024]{1,0:T(8,128)(2,1)S(1)} %fusion.68), channel_id=1, source_target_pairs={{8,0},{16,8},{24,16},{28,24},{20,28},{12,20},{4,12},{0,4},{9,1},{1... | collective-permute-start | bytes 786440 | tf_op jit(solution)/shard_map/ppermute | solution.py:325
  218.6 73.4 %reduce-scatter.6.cloned.1.call-start = ((), (), s32[]{:S(2)}) async-start(), calls=%async_computation.10 | async-start | bytes 1679360 | tf_op jit(solution)/shard_map/reduce_scatter | solution.py:429
  253.1 64.0 %reduce-scatter.4.cloned.1.call-start = ((), (), s32[]{:S(2)}) async-start(), calls=%async_computation.9 | async-start | bytes 1310720 | tf_op jit(solution)/shard_map/reduce_scatter | solution.py:488
  291.3 72.5 %all-gather.12.cloned.1.call-start = ((), (), s32[]{:S(2)}) async-start(), calls=%async_computation.12 | async-start | bytes 1511424 | tf_op jit(solution)/shard_map/all_gather | solution.py:437
  291.9 127.4 %all-gather.16.cloned.1.call-start = ((), (), s32[]{:S(2)}) async-start(), calls=%async_computation.14 | async-start | bytes 3022848 | tf_op jit(solution)/shard_map/all_gather | solution.py:430
  292.7 176.5 %all-gather.14.cloned.1.call-start = ((), (), s32[]{:S(2)}) async-start(), calls=%async_computation.13 | async-start | bytes 2359296 | tf_op jit(solution)/shard_map/all_gather | solution.py:489
  327.5 11.1 %collective-permute-start.54 = (bf16[128,1024]{1,0:T(8,128)(2,1)S(1)}, bf16[128,1024]{1,0:T(8,128)(2,1)S(1)}, u32[]{:S(2)}, u32[]{:S(2)}) collective-permute-start(bf16[128,1024]{1,0:T(8,128)(2,1)S(1)} %fusion.59), channel_id=1, source_target_pairs={{8,0},{16,8},{24,16},{28,24},{20,28},{12,20},{4,12},{0,4},{9,1},{1... | collective-permute-start | bytes 786440 | tf_op jit(solution)/shard_map/ppermute | solution.py:325
  329.2 43.1 %collective-permute-start.51 = (bf16[128,1024]{1,0:T(8,128)(2,1)S(1)}, bf16[128,1024]{1,0:T(8,128)(2,1)}, u32[]{:S(2)}, u32[]{:S(2)}) collective-permute-start(bf16[128,1024]{1,0:T(8,128)(2,1)S(1)} %get-tuple-element.56), channel_id=1, source_target_pairs={{0,8},{8,16},{16,24},{24,28},{28,20},{20,12},{12,4},{4,0},{1,9},{9... | collective-permute-start | bytes 786440 | tf_op jit(solution)/shard_map/ppermute | solution.py:324
  340.4 31.8 %collective-permute-start.55 = (bf16[128,1024]{1,0:T(8,128)(2,1)}, bf16[128,1024]{1,0:T(8,128)(2,1)}, u32[]{:S(2)}, u32[]{:S(2)}) collective-permute-start(bf16[128,1024]{1,0:T(8,128)(2,1)} %fusion.60), channel_id=1, source_target_pairs={{8,0},{16,8},{24,16},{28,24},{20,28},{12,20},{4,12},{0,4},{9,1},{1... | collective-permute-start | bytes 786440 | tf_op jit(solution)/shard_map/ppermute | solution.py:325
  363.9 22.1 %all-to-all-start.3 = ((bf16[4,656,256]{2,1,0:T(8,128)(2,1)}), bf16[4,656,256]{2,1,0:T(8,128)(2,1)}, u32[]{:S(2)}, u32[]{:S(2)}) async-start(bf16[4,656,256]{2,1,0:T(8,128)(2,1)} %bitcast.156), calls=%async_computation.6 | async-start | bytes 2686976 | tf_op jit(solution)/shard_map/all_to_all | solution.py:438
  475.6 13.0 %all-to-all-start.2 = ((bf16[4,256,256]{2,1,0:T(8,128)(2,1)}), bf16[4,256,256]{2,1,0:T(8,128)(2,1)}, u32[]{:S(2)}, u32[]{:S(2)}) async-start(bf16[4,256,256]{2,1,0:T(8,128)(2,1)} %bitcast.151), calls=%async_computation.3 | async-start | bytes 1048576 | tf_op jit(solution)/shard_map/all_to_all | solution.py:493
  (79 other events, 724.8 us)
Sparse Core Ops, SparseCore 0:
  9.6 29.3 all-gather.7
  40.5 19.8 all-gather.9
  218.7 23.5 reduce-scatter.7
  253.2 26.9 reduce-scatter.5
  291.4 25.5 reduce-scatter.3
  319.1 44.6 all-gather.11
  366.0 53.2 all-gather.15
  421.4 47.6 all-gather.13

commit v3 on v2

--- a/solution.py
+++ b/solution.py
@@ -287,7 +287,7 @@
 
 def gather_tokens(rows):
     blocks = lax.axis_size("ctx")
-    half, cut = blocks // 2, rows.shape[0] // 2
+    half, cut = blocks // 2, rows.shape[0] // 32 * 16
     ahead, behind = ring_moves(blocks)
     found = [rows] + [None] * (blocks - 1)
     from_before = from_after = rows
@@ -360,7 +360,8 @@
         ],
         axis=1,
     )
-    packed = jnp.concatenate([qkv_part, gain_one[:, None], gain_two[:, None]], axis=1)
+    gains = jnp.pad(jnp.stack([gain_one, gain_two], axis=1), ((0, 0), (0, 126)))
+    packed = jnp.concatenate([qkv_part, gains], axis=1)
     packed = lax.all_gather(packed, "fsdp", axis=0, tiled=True)
     qkv_c = packed[:, : 3 * head_cols]
     full_g1 = packed[:, 3 * head_cols].astype(f32)
@@ -375,7 +376,8 @@
         axis=1,
         tiled=True,
     )
-    all_cot = gather_tokens(own_cot)
+    all_x, later_cot = lax.optimization_barrier((all_x, own_cot))
+    all_cot = gather_tokens(later_cot)
 
     normed_all, _ = norm_parts(all_x.astype(f32))
     input_one = (normed_all * full_g1).astype(bf16)
@@ -418,29 +420,33 @@
     grad_wide = jnp.concatenate(
         [grad_hidden * gating * gelu_slope(inner_part), grad_hidden * activated], axis=-1
     ).astype(bf16)
-    own_grad_two = scatter_tokens(
-        lax.dot_general(grad_wide, in_c, (((1,), (1,)), ((), ())), preferred_element_type=f32)
-    )
-    output = resid + scatter_tokens(jnp.dot(hidden, ffn_c, preferred_element_type=f32))
-
+    grad_ffn = lax.dot_general(
+        hidden, all_cot, (((0,), (0,)), ((), ())), preferred_element_type=f32
+    ).astype(bf16)
     grad_in = lax.dot_general(
         grad_wide, input_two, (((0,), (0,)), ((), ())), preferred_element_type=f32
     ).astype(bf16)
+    part_two = lax.dot_general(
+        grad_wide, in_c, (((1,), (1,)), ((), ())), preferred_element_type=f32
+    )
+    part_two, grad_ffn, grad_in = lax.optimization_barrier((part_two, grad_ffn, grad_in))
+    grad_ffn = lax.psum_scatter(grad_ffn, "fsdp", scatter_dimension=1, tiled=True)
     grad_in = lax.psum_scatter(grad_in, "fsdp", scatter_dimension=1, tiled=True)
     grad_in = lax.all_gather(grad_in, "ctx", axis=0, tiled=False)
     grad_in = grad_in.reshape(blocks, 2, unit_dev, row_part).transpose(1, 0, 2, 3)
     grad_in = grad_in.reshape(2 * FF, row_part).T.astype(f32)
-    grad_ffn = lax.dot_general(
-        hidden, all_cot, (((0,), (0,)), ((), ())), preferred_element_type=f32
-    ).astype(bf16)
-    grad_ffn = lax.psum_scatter(grad_ffn, "fsdp", scatter_dimension=1, tiled=True)
-    grad_ffn = lax.all_gather(grad_ffn, "ctx", axis=0, tiled=True)
-    grad_ffn = lax.all_to_all(grad_ffn, "fsdp", split_axis=0, concat_axis=1, tiled=True)
-    grad_ffn = grad_ffn.astype(f32)
+    own_grad_two = scatter_tokens(part_two)
 
     own_resid = own_cot.astype(f32) + norm_back(own_grad_two * full_g2, normed_two, inv_two)
     resid_b = own_resid.astype(bf16)
     all_resid = gather_tokens(resid_b)
+    all_resid, later_hidden, grad_ffn = lax.optimization_barrier((all_resid, hidden, grad_ffn))
+    output = resid + scatter_tokens(jnp.dot(later_hidden, ffn_c, preferred_element_type=f32))
+    block_of = (places - place) % blocks
+    grad_ffn = jnp.take(gather_tokens(grad_ffn).reshape(blocks, unit_dev, -1), block_of, axis=0)
+    grad_ffn = grad_ffn.reshape(FF, row_part)
+    grad_ffn = lax.all_to_all(grad_ffn, "fsdp", split_axis=0, concat_axis=1, tiled=True)
+    grad_ffn = grad_ffn.astype(f32)
     attn_c = lax.dynamic_slice_in_dim(full_attn, block * head_cols, head_cols, 0)
     mixed = lax.dot_general(
         all_resid, attn_c, (((1,), (1,)), ((), ())), preferred_element_type=f32
@@ -486,7 +492,7 @@
     ).astype(bf16)
     grads = jnp.concatenate([grad_qkv, grad_attn])
     grads = lax.psum_scatter(grads, "fsdp", scatter_dimension=1, tiled=True)
-    grads = lax.all_gather(grads, "ctx", axis=0, tiled=False)
+    grads = jnp.take(gather_tokens(grads).reshape(blocks, -1, row_part), block_of, axis=0)
     grad_qkv = grads[:, : 3 * head_cols].reshape(blocks, 3, head_cols, row_part)
     grad_qkv = grad_qkv.transpose(1, 0, 2, 3).reshape(3 * D, row_part).T.astype(f32)
     grad_attn = grads[:, 3 * head_cols :].reshape(D, row_part)

time: 503 us -> 483 us (0.960)
  waiting for transfers between devices: 214 us -> 131 us
  starting transfers between devices: 81.5 us -> 107 us
  local copies, waits for them, and re-layouts: 86.1 us -> 111 us
  other arithmetic: 39.1 us -> 60.8 us
  blocking collectives: 21.2 us -> 7.85 us
    all_gather x2 -> x1, waiting for transfers between devices: 56.9 us -> 0.02 us  [by_heads(): packed = lax.all_gather(packed, 'fsdp', axis=0, tiled=True)]
    all_gather x1, waiting for transfers between devices: 29.8 us -> 0.01 us  [by_heads(): grad_in = lax.all_gather(grad_in, 'ctx', axis=0, tiled=False)]
    ppermute x12 -> x18, waiting for transfers between devices: 16.3 us -> 36.4 us  [gather_tokens(): from_before = lax.ppermute(from_before, 'ctx', ahead)]
    ppermute x4 -> x6, waiting for transfers between devices: 3.34 us -> 18.3 us  [gather_tokens(): lax.ppermute(from_before[:cut], 'ctx', ahead)]
    unnamed x120 -> x128, local copies, waits for them, and re-layouts: 37.8 us -> 51.6 us
    all_gather x1 -> x0, blocking collectives: 13.3 us -> none  [by_heads(): packed = lax.all_gather(packed, 'fsdp', axis=0, tiled=True)]
    ppermute x12 -> x18, starting transfers between devices: 18.2 us -> 30.8 us  [gather_tokens(): from_after = lax.ppermute(from_after, 'ctx', behind)]
    ppermute x9, waiting for transfers between devices: 19.1 us -> 7.06 us  [scatter_tokens(): to_ahead = lax.ppermute(to_ahead, 'ctx', ahead)]
  transfers between devices with their start and end apart: 68 -> 83, of which waited for: 40 -> 39; matrix products, arithmetic and copies ran while one was open for 28% -> 36% of each run, Pallas kernels for 0% -> 0%
where the time goes in v3:
time: 483 us; the launch traced here: 478 us
  waiting for transfers between devices  131 us (27%)
  local copies, waits for them, and re-layouts  111 us (23%)
  starting transfers between devices  107 us (22%)
  other arithmetic  60.8 us (13%)
  matrix products  44.3 us (9%)
  between operations  15.4 us (3%)
  blocking collectives  7.85 us (2%)
    unnamed x128, local copies, waits for them, and re-layouts  51.6 us
    ppermute x18, waiting for transfers between devices, gather_tokens(): from_before = lax.ppermute(from_before, 'ctx', ahead)  36.4 us
    ppermute x9, waiting for transfers between devices, scatter_tokens(): to_behind = lax.ppermute(to_behind, 'ctx', behind)  32.9 us
    ppermute x18, starting transfers between devices, gather_tokens(): from_after = lax.ppermute(from_after, 'ctx', behind)  30.8 us
    ppermute x6, waiting for transfers between devices, gather_tokens(): lax.ppermute(from_before[:cut], 'ctx', ahead)  18.3 us
    ppermute x9, starting transfers between devices, scatter_tokens(): to_ahead = lax.ppermute(to_ahead, 'ctx', ahead)  14.2 us
    ppermute x18, waiting for transfers between devices, gather_tokens(): from_after = lax.ppermute(from_after, 'ctx', behind)  12.4 us
    ppermute x6, starting transfers between devices, gather_tokens(): lax.ppermute(from_after[cut:], 'ctx', behind)  12.4 us
  transfers between devices with their start and end apart: 83, of which 39 were waited for; matrix products, arithmetic and copies ran while one was open for 36% of the time, Pallas kernels for 0%

profile of v3, /device:TPU:0, one launch (start us, length us, event | category | flops | bytes accessed | tf_op | source)
XLA Modules:
  0.0 477.9 jit_solution(16908414718275382886)
XLA Ops:
  16.3 4.4 all-to-all-start.1
  29.0 6.8 %collective-permute-done.4 = bf16[128,1024]{1,0:T(8,128)(2,1)} collective-permute-done((bf16[128,1024]{1,0:T(8,128)(2,1)S(1)}, bf16[128,1024]{1,0:T(8,128)(2,1)}, u32[]{:S(2)}, u32[]{:S(2)}) %collective-permute-start.4) | collective-permute-done | bytes 262176 | tf_op jit(solution)/shard_map/ppermute | solution.py:295
  37.9 5.5 %collective-permute-done.5 = bf16[128,1024]{1,0:T(8,128)(2,1)S(1)} collective-permute-done((bf16[128,1024]{1,0:T(8,128)(2,1)}, bf16[128,1024]{1,0:T(8,128)(2,1)S(1)}, u32[]{:S(2)}, u32[]{:S(2)}) %collective-permute-start.5) | collective-permute-done | bytes 262176 | tf_op jit(solution)/shard_map/ppermute | solution.py:295
  81.3 5.6 %all-to-all-start = ((bf16[8,128,128]{2,1,0:T(8,128)(2,1)}), bf16[8,128,128]{2,1,0:T(8,128)(2,1)S(1)}, u32[]{:S(2)}, u32[]{:S(2)}) async-start(bf16[8,128,128]{2,1,0:T(8,128)(2,1)} %broadcast_select_fusion.1), calls=%async_computation | async-start | bytes 524288 | tf_op jit(solution)/shard_map/all_to_all | solution.py:405
  91.7 7.8 %all_gather.20 = bf16[328,1024]{1,0:T(8,128)(2,1)S(1)} all-gather(bf16[328,256]{1,0:T(8,128)(2,1)S(1)} %constant_dynamic-slice_fusion.2), channel_id=1, replica_groups=mesh['ctx'=8,'fsdp'=4] {'fsdp'}, dimensions={1}, use_global_device_ids=true | all-gather | bytes 839680 | tf_op jit(solution)/shard_map/all_gather | solution.py:373
  140.3 3.8 fusion.107
  144.1 5.2 %multiply_convert_fusion.1 = (bf16[1024,328]{0,1:T(8,128)(2,1)S(1)}, f32[1024,328]{0,1:T(8,128)S(1)}, bf16[1024,328]{0,1:T(8,128)(2,1)}, f32[1024,328]{0,1:T(8,128)}) fusion(f32[1024,656]{0,1:T(8,128)S(1)} %fusion.107, bf16[1024,1024]{1,0:T(8,128)(2,1)S(1)} %copy-done.34, bf16[328,1024]{1,0:T(8,128)(2,1)S(1)} %all_gather.20), kind=kOutput, calls=%fused_computation.46 | convolution fusion | flops 713728000 | bytes 9486336 | tf_op jit(solution)/shard_map/dot_general | solution.py:417
  153.4 4.5 convolution_convert_fusion
  163.2 4.8 %collective-permute-done.24 = bf16[64,1024]{1,0:T(8,128)(2,1)S(1)} collective-permute-done((bf16[64,1024]{1,0:T(8,128)(2,1)S(1)}, bf16[64,1024]{1,0:T(8,128)(2,1)S(1)}, u32[]{:S(2)}, u32[]{:S(2)}) %collective-permute-start.24) | collective-permute-done | bytes 131104 | tf_op jit(solution)/shard_map/ppermute | solution.py:315
  169.6 7.0 %collective-permute-done.25 = bf16[128,1024]{1,0:T(8,128)(2,1)S(1)} collective-permute-done((bf16[128,1024]{1,0:T(8,128)(2,1)S(1)}, bf16[128,1024]{1,0:T(8,128)(2,1)S(1)}, u32[]{:S(2)}, u32[]{:S(2)}) %collective-permute-start.25) | collective-permute-done | bytes 262176 | tf_op jit(solution)/shard_map/ppermute | solution.py:324
  178.8 4.6 collective-permute-done.28
  184.8 5.6 %collective-permute-done.29 = bf16[128,1024]{1,0:T(8,128)(2,1)S(1)} collective-permute-done((bf16[128,1024]{1,0:T(8,128)(2,1)S(1)}, bf16[128,1024]{1,0:T(8,128)(2,1)S(1)}, u32[]{:S(2)}, u32[]{:S(2)}) %collective-permute-start.29) | collective-permute-done | bytes 262176 | tf_op jit(solution)/shard_map/ppermute | solution.py:325
  192.5 4.3 collective-permute-done.30
  198.7 6.5 %collective-permute-done.31 = bf16[128,1024]{1,0:T(8,128)(2,1)S(1)} collective-permute-done((bf16[128,1024]{1,0:T(8,128)(2,1)S(1)}, bf16[128,1024]{1,0:T(8,128)(2,1)S(1)}, u32[]{:S(2)}, u32[]{:S(2)}) %collective-permute-start.31) | collective-permute-done | bytes 262176 | tf_op jit(solution)/shard_map/ppermute | solution.py:325
  211.2 4.8 %collective-permute-done.32 = bf16[128,1024]{1,0:T(8,128)(2,1)S(1)} collective-permute-done((bf16[128,1024]{1,0:T(8,128)(2,1)S(1)}, bf16[128,1024]{1,0:T(8,128)(2,1)S(1)}, u32[]{:S(2)}, u32[]{:S(2)}) %collective-permute-start.32) | collective-permute-done | bytes 262176 | tf_op jit(solution)/shard_map/ppermute | solution.py:296
  219.2 3.3 collective-permute-done.33
  228.9 4.5 collective-permute-done.37
  251.9 3.5 multiply_convert_fusion
  262.2 3.8 fusion.37
  270.8 3.5 copy.104
  279.4 3.7 copy.107
  321.7 12.8 %collective-permute-done.70 = bf16[160,256]{1,0:T(8,128)(2,1)S(1)} collective-permute-done((bf16[160,256]{1,0:T(8,128)(2,1)S(1)}, bf16[160,256]{1,0:T(8,128)(2,1)S(1)}, u32[]{:S(2)}, u32[]{:S(2)}) %collective-permute-start.70) | collective-permute-done | bytes 81952 | tf_op jit(solution)/shard_map/ppermute | solution.py:301
  351.0 13.6 %collective-permute-done.53 = bf16[128,1024]{1,0:T(8,128)(2,1)S(1)} collective-permute-done((bf16[128,1024]{1,0:T(8,128)(2,1)S(1)}, bf16[128,1024]{1,0:T(8,128)(2,1)S(1)}, u32[]{:S(2)}, u32[]{:S(2)}) %collective-permute-start.53) | collective-permute-done | bytes 262176 | tf_op jit(solution)/shard_map/ppermute | solution.py:325
  381.2 4.3 all-to-all-start.3
  396.9 4.5 collective-permute-done.59
  405.5 3.8 collective-permute-done.60
  428.0 3.6 gather_fusion.2
  438.6 4.1 all-to-all-start.2
  442.7 4.6 multiply_reduce_fusion.2
  447.9 3.7 all-to-all-done.2
  456.4 4.6 copy.108
  461.0 6.0 %copy.111 = f32[256,5248]{1,0:T(8,128)} copy(f32[256,5248]{0,1:T(8,128)} %bitcast.136) | data formatting | bytes 10747904
  (424 shorter events, 293.0 us)
Async XLA Ops:
  7.2 47.4 %all-gather.6.cloned.1.call-start = ((), (), s32[]{:S(2)}) async-start(), calls=%async_computation.7 | async-start | bytes 1310720 | tf_op jit(solution)/shard_map/all_gather | solution.py:365
  9.8 91.9 %all-gather.8.cloned.1.call-start = ((), (), s32[]{:S(2)}) async-start(), calls=%async_computation.8 | async-start | bytes 2621440 | tf_op jit(solution)/shard_map/all_gather | solution.py:370
  10.6 14.8 %collective-permute-start = (bf16[128,1024]{1,0:T(8,128)(2,1)S(1)}, bf16[128,1024]{1,0:T(8,128)(2,1)S(1)}, u32[]{:S(2)}, u32[]{:S(2)}) collective-permute-start(bf16[128,1024]{1,0:T(8,128)(2,1)S(1)} %bitcast.140), channel_id=1, source_target_pairs={{8,0},{16,8},{24,16},{28,24},{20,28},{12,20},{4,12},{0,4},{9,1},{1... | collective-permute-start | bytes 786440 | tf_op jit(solution)/shard_map/ppermute | solution.py:296
  13.6 13.7 %collective-permute-start.3 = (bf16[128,1024]{1,0:T(8,128)(2,1)S(1)}, bf16[128,1024]{1,0:T(8,128)(2,1)S(1)}, u32[]{:S(2)}, u32[]{:S(2)}) collective-permute-start(bf16[128,1024]{1,0:T(8,128)(2,1)S(1)} %bitcast.141), channel_id=1, source_target_pairs={{0,8},{8,16},{16,24},{24,28},{28,20},{20,12},{12,4},{4,0},{1,9},{9... | collective-permute-start | bytes 786440 | tf_op jit(solution)/shard_map/ppermute | solution.py:295
  16.3 65.1 %all-to-all-start.1 = ((bf16[656,4,256]{2,0,1:T(8,128)(2,1)}), bf16[656,4,256]{2,0,1:T(8,128)(2,1)}, u32[]{:S(2)}, u32[]{:S(2)}) async-start(bf16[656,4,256]{2,0,1:T(8,128)(2,1)} %bitcast.134), calls=%async_computation.1 | async-start | bytes 2686976 | tf_op jit(solution)/shard_map/all_to_all | solution.py:372
  20.7 119.6 %all-gather.10.cloned.1.call-start = ((), (), s32[]{:S(2)}) async-start(), calls=%async_computation.9 | async-start | bytes 1966080 | tf_op jit(solution)/shard_map/all_gather | solution.py:371
  51.3 37.4 %collective-permute-start.8 = (bf16[128,1024]{1,0:T(8,128)(2,1)}, bf16[128,1024]{1,0:T(8,128)(2,1)}, u32[]{:S(2)}, u32[]{:S(2)}) collective-permute-start(bf16[128,1024]{1,0:T(8,128)(2,1)} %bitcast.2), channel_id=1, source_target_pairs={{8,0},{16,8},{24,16},{28,24},{20,28},{12,20},{4,12},{0,4},{9,1},{1... | collective-permute-start | bytes 786440 | tf_op jit(solution)/shard_map/ppermute | solution.py:296
  52.6 38.0 %collective-permute-start.11 = (bf16[128,1024]{1,0:T(8,128)(2,1)}, bf16[128,1024]{1,0:T(8,128)(2,1)}, u32[]{:S(2)}, u32[]{:S(2)}) collective-permute-start(bf16[128,1024]{1,0:T(8,128)(2,1)} %bitcast.2), channel_id=1, source_target_pairs={{0,8},{8,16},{16,24},{24,28},{28,20},{20,12},{12,4},{4,0},{1,9},{9... | collective-permute-start | bytes 786440 | tf_op jit(solution)/shard_map/ppermute | solution.py:295
  81.3 20.2 %all-to-all-start = ((bf16[8,128,128]{2,1,0:T(8,128)(2,1)}), bf16[8,128,128]{2,1,0:T(8,128)(2,1)S(1)}, u32[]{:S(2)}, u32[]{:S(2)}) async-start(bf16[8,128,128]{2,1,0:T(8,128)(2,1)} %broadcast_select_fusion.1), calls=%async_computation | async-start | bytes 524288 | tf_op jit(solution)/shard_map/all_to_all | solution.py:405
  87.0 157.5 %reduce-scatter.4.cloned.1.call-start = ((), (), s32[]{:S(2)}) async-start(), calls=%async_computation.10 | async-start | bytes 839680 | tf_op jit(solution)/shard_map/reduce_scatter | solution.py:433
  99.5 14.2 %collective-permute-start.10 = (bf16[128,1024]{1,0:T(8,128)(2,1)}, bf16[128,1024]{1,0:T(8,128)(2,1)S(1)}, u32[]{:S(2)}, u32[]{:S(2)}) collective-permute-start(bf16[128,1024]{1,0:T(8,128)(2,1)} %collective-permute-done.9), channel_id=1, source_target_pairs={{8,0},{16,8},{24,16},{28,24},{20,28},{12,20},{4,12},{0,4},{9,1},{1... | collective-permute-start | bytes 786440 | tf_op jit(solution)/shard_map/ppermute | solution.py:296
  105.2 11.1 %collective-permute-start.19 = (bf16[128,1024]{1,0:T(8,128)(2,1)S(1)}, bf16[128,1024]{1,0:T(8,128)(2,1)S(1)}, u32[]{:S(2)}, u32[]{:S(2)}) collective-permute-start(bf16[128,1024]{1,0:T(8,128)(2,1)S(1)} %get-tuple-element.69), channel_id=1, source_target_pairs={{0,8},{8,16},{16,24},{24,28},{28,20},{20,12},{12,4},{4,0},{1,9},{9... | collective-permute-start | bytes 786440 | tf_op jit(solution)/shard_map/ppermute | solution.py:295
  198.6 107.6 %reduce-scatter.8.cloned.1.call-start = ((), (), s32[]{:S(2)}) async-start(), calls=%async_computation.12 | async-start | bytes 1679360 | tf_op jit(solution)/shard_map/reduce_scatter | solution.py:434
  222.5 13.1 %collective-permute-start.34 = (bf16[128,1024]{1,0:T(8,128)(2,1)}, bf16[128,1024]{1,0:T(8,128)(2,1)}, u32[]{:S(2)}, u32[]{:S(2)}) collective-permute-start(bf16[128,1024]{1,0:T(8,128)(2,1)} %collective-permute-done.33), channel_id=1, source_target_pairs={{8,0},{16,8},{24,16},{28,24},{20,28},{12,20},{4,12},{0,4},{9,1},{1... | collective-permute-start | bytes 786440 | tf_op jit(solution)/shard_map/ppermute | solution.py:296
  227.9 164.2 %reduce-scatter.6.cloned.1.call-start = ((), (), s32[]{:S(2)}) async-start(), calls=%async_computation.11 | async-start | bytes 1310720 | tf_op jit(solution)/shard_map/reduce_scatter | solution.py:494
  279.2 177.2 %all-gather.12.cloned.1.call-start = ((), (), s32[]{:S(2)}) async-start(), calls=%async_computation.13 | async-start | bytes 3022848 | tf_op jit(solution)/shard_map/all_gather | solution.py:435
  283.4 18.5 %collective-permute-start.64 = (bf16[328,256]{1,0:T(8,128)(2,1)}, bf16[328,256]{1,0:T(8,128)(2,1)}, u32[]{:S(2)}, u32[]{:S(2)}) collective-permute-start(bf16[328,256]{1,0:T(8,128)(2,1)} %reduce-scatter.4.cloned.1.call-done), channel_id=1, source_target_pairs={{8,0},{16,8},{24,16},{28,24},{20,28},{12,20},{4,12},{0,4},{9,1},{1... | collective-permute-start | bytes 503816 | tf_op jit(solution)/shard_map/ppermute | solution.py:296
  285.3 17.3 %collective-permute-start.67 = (bf16[328,256]{1,0:T(8,128)(2,1)}, bf16[328,256]{1,0:T(8,128)(2,1)}, u32[]{:S(2)}, u32[]{:S(2)}) collective-permute-start(bf16[328,256]{1,0:T(8,128)(2,1)} %reduce-scatter.4.cloned.1.call-done), channel_id=1, source_target_pairs={{0,8},{8,16},{16,24},{24,28},{28,20},{20,12},{12,4},{4,0},{1,9},{9... | collective-permute-start | bytes 503816 | tf_op jit(solution)/shard_map/ppermute | solution.py:295
  291.4 49.7 %collective-permute-start.52 = (bf16[64,1024]{1,0:T(8,128)(2,1)}, bf16[64,1024]{1,0:T(8,128)(2,1)}, u32[]{:S(2)}, u32[]{:S(2)}) collective-permute-start(bf16[64,1024]{1,0:T(8,128)(2,1)} %get-tuple-element.84), channel_id=1, source_target_pairs={{8,0},{16,8},{24,16},{28,24},{20,28},{12,20},{4,12},{0,4},{9,1},{1... | collective-permute-start | bytes 393224 | tf_op jit(solution)/shard_map/ppermute | solution.py:316
  296.2 51.0 %collective-permute-start.44 = (bf16[64,1024]{1,0:T(8,128)(2,1)}, bf16[64,1024]{1,0:T(8,128)(2,1)}, u32[]{:S(2)}, u32[]{:S(2)}) collective-permute-start(bf16[64,1024]{1,0:T(8,128)(2,1)} %get-tuple-element.86), channel_id=1, source_target_pairs={{8,0},{16,8},{24,16},{28,24},{20,28},{12,20},{4,12},{0,4},{9,1},{1... | collective-permute-start | bytes 393224 | tf_op jit(solution)/shard_map/ppermute | solution.py:316
  299.8 13.1 %collective-permute-start.49 = (bf16[128,1024]{1,0:T(8,128)(2,1)}, bf16[128,1024]{1,0:T(8,128)(2,1)}, u32[]{:S(2)}, u32[]{:S(2)}) collective-permute-start(bf16[128,1024]{1,0:T(8,128)(2,1)} %fusion.61), channel_id=1, source_target_pairs={{0,8},{8,16},{16,24},{24,28},{28,20},{20,12},{12,4},{4,0},{1,9},{9... | collective-permute-start | bytes 786440 | tf_op jit(solution)/shard_map/ppermute | solution.py:324
  314.7 26.4 %collective-permute-start.50 = (bf16[128,1024]{1,0:T(8,128)(2,1)S(1)}, bf16[128,1024]{1,0:T(8,128)(2,1)S(1)}, u32[]{:S(2)}, u32[]{:S(2)}) collective-permute-start(bf16[128,1024]{1,0:T(8,128)(2,1)S(1)} %fusion.62), channel_id=1, source_target_pairs={{0,8},{8,16},{16,24},{24,28},{28,20},{20,12},{12,4},{4,0},{1,9},{9... | collective-permute-start | bytes 786440 | tf_op jit(solution)/shard_map/ppermute | solution.py:324
  318.5 28.7 %collective-permute-start.42 = (bf16[128,1024]{1,0:T(8,128)(2,1)S(1)}, bf16[128,1024]{1,0:T(8,128)(2,1)S(1)}, u32[]{:S(2)}, u32[]{:S(2)}) collective-permute-start(bf16[128,1024]{1,0:T(8,128)(2,1)S(1)} %fusion.70), channel_id=1, source_target_pairs={{0,8},{8,16},{16,24},{24,28},{28,20},{20,12},{12,4},{4,0},{1,9},{9... | collective-permute-start | bytes 786440 | tf_op jit(solution)/shard_map/ppermute | solution.py:324
  319.1 15.5 %collective-permute-start.70 = (bf16[160,256]{1,0:T(8,128)(2,1)S(1)}, bf16[160,256]{1,0:T(8,128)(2,1)S(1)}, u32[]{:S(2)}, u32[]{:S(2)}) collective-permute-start(bf16[160,256]{1,0:T(8,128)(2,1)S(1)} %slice.303), channel_id=1, source_target_pairs={{0,8},{8,16},{16,24},{24,28},{28,20},{20,12},{12,4},{4,0},{1,9},{9... | collective-permute-start | bytes 245768 | tf_op jit(solution)/shard_map/ppermute | solution.py:301
  343.2 21.4 %collective-permute-start.53 = (bf16[128,1024]{1,0:T(8,128)(2,1)S(1)}, bf16[128,1024]{1,0:T(8,128)(2,1)S(1)}, u32[]{:S(2)}, u32[]{:S(2)}) collective-permute-start(bf16[128,1024]{1,0:T(8,128)(2,1)S(1)} %get-tuple-element.73), channel_id=1, source_target_pairs={{8,0},{16,8},{24,16},{28,24},{20,28},{12,20},{4,12},{0,4},{9,1},{1... | collective-permute-start | bytes 786440 | tf_op jit(solution)/shard_map/ppermute | solution.py:325
  349.3 25.4 %collective-permute-start.45 = (bf16[128,1024]{1,0:T(8,128)(2,1)}, bf16[128,1024]{1,0:T(8,128)(2,1)}, u32[]{:S(2)}, u32[]{:S(2)}) collective-permute-start(bf16[128,1024]{1,0:T(8,128)(2,1)} %get-tuple-element.75), channel_id=1, source_target_pairs={{8,0},{16,8},{24,16},{28,24},{20,28},{12,20},{4,12},{0,4},{9,1},{1... | collective-permute-start | bytes 786440 | tf_op jit(solution)/shard_map/ppermute | solution.py:325
  366.4 11.4 %collective-permute-start.54 = (bf16[128,1024]{1,0:T(8,128)(2,1)}, bf16[128,1024]{1,0:T(8,128)(2,1)}, u32[]{:S(2)}, u32[]{:S(2)}) collective-permute-start(bf16[128,1024]{1,0:T(8,128)(2,1)} %fusion.59), channel_id=1, source_target_pairs={{8,0},{16,8},{24,16},{28,24},{20,28},{12,20},{4,12},{0,4},{9,1},{1... | collective-permute-start | bytes 786440 | tf_op jit(solution)/shard_map/ppermute | solution.py:325
  371.0 18.9 %collective-permute-start.51 = (bf16[128,1024]{1,0:T(8,128)(2,1)}, bf16[128,1024]{1,0:T(8,128)(2,1)}, u32[]{:S(2)}, u32[]{:S(2)}) collective-permute-start(bf16[128,1024]{1,0:T(8,128)(2,1)} %get-tuple-element.72), channel_id=1, source_target_pairs={{0,8},{8,16},{16,24},{24,28},{28,20},{20,12},{12,4},{4,0},{1,9},{9... | collective-permute-start | bytes 786440 | tf_op jit(solution)/shard_map/ppermute | solution.py:324
  381.2 28.4 %all-to-all-start.3 = ((bf16[4,656,256]{2,1,0:T(8,128)(2,1)}), bf16[4,656,256]{2,1,0:T(8,128)(2,1)}, u32[]{:S(2)}, u32[]{:S(2)}) async-start(bf16[4,656,256]{2,1,0:T(8,128)(2,1)} %bitcast_select_fusion), calls=%async_computation.6 | async-start | bytes 2686976 | tf_op jit(solution)/shard_map/all_to_all | solution.py:448
  385.5 16.5 %collective-permute-start.43 = (bf16[128,1024]{1,0:T(8,128)(2,1)}, bf16[128,1024]{1,0:T(8,128)(2,1)}, u32[]{:S(2)}, u32[]{:S(2)}) collective-permute-start(bf16[128,1024]{1,0:T(8,128)(2,1)} %get-tuple-element.74), channel_id=1, source_target_pairs={{0,8},{8,16},{16,24},{24,28},{28,20},{20,12},{12,4},{4,0},{1,9},{9... | collective-permute-start | bytes 786440 | tf_op jit(solution)/shard_map/ppermute | solution.py:324
  389.4 12.6 %collective-permute-start.47 = (bf16[128,1024]{1,0:T(8,128)(2,1)}, bf16[128,1024]{1,0:T(8,128)(2,1)}, u32[]{:S(2)}, u32[]{:S(2)}) collective-permute-start(bf16[128,1024]{1,0:T(8,128)(2,1)} %fusion.68), channel_id=1, source_target_pairs={{8,0},{16,8},{24,16},{28,24},{20,28},{12,20},{4,12},{0,4},{9,1},{1... | collective-permute-start | bytes 786440 | tf_op jit(solution)/shard_map/ppermute | solution.py:325
  438.6 13.0 %all-to-all-start.2 = ((bf16[4,256,256]{2,1,0:T(8,128)(2,1)}), bf16[4,256,256]{2,1,0:T(8,128)(2,1)}, u32[]{:S(2)}, u32[]{:S(2)}) async-start(bf16[4,256,256]{2,1,0:T(8,128)(2,1)} %bitcast.25), calls=%async_computation.4 | async-start | bytes 1048576 | tf_op jit(solution)/shard_map/all_to_all | solution.py:499
  (90 other events, 630.7 us)
Sparse Core Ops, SparseCore 0:
  10.1 23.9 all-gather.5
  35.6 22.0 all-gather.7
  59.3 19.6 all-gather.9
  198.7 23.6 reduce-scatter.3
  228.0 29.4 reduce-scatter.7
  279.3 27.0 reduce-scatter.5
  308.6 67.2 all-gather.11
